TPU v7x, 1024 devices: a whole 4x4x32 slice. The times are simulated.
1024 devices in a mesh: seq: 64 (over z, core), head: 16 (over y, x).
Axes of the slice: x: 4, y: 4, z: 32, core: 2. Of those that a mesh axis runs over, the one named last changes fastest.
Arguments:
- queries: bfloat16 [16384, 8192], P('seq', 'head'), may hold values from -6 to 6
- key_input: bfloat16 [16384, 8192], P('seq', 'head'), may hold values from -6 to 6
- value_input: bfloat16 [16384, 8192], P('seq', 'head'), may hold values from -6 to 6
- out_gate: bfloat16 [16384, 8192], P('seq', 'head'), may hold values from -8 to 8
- log_decay: float32 [64, 16384], P('head', 'seq'), may hold values from -1 to 0, as said below
- norm_gain: float32 [8192], P('head'), may hold values from 0.1 to 1.9
- features: bfloat16 [16384, 6144], P('seq', 'head'), may hold values from -6 to 6
- expert_ids: int32 [16384, 2], P('seq'), may hold values from 0 to 31, as said below
- route_weight: float32 [16384, 2], P('seq'), may hold values from 0.25 to 1
- placement: int32 [4], replicated, may hold values from 0 to 31, as said below
- gate_weight: bfloat16 [6144, 36864], P('head', 'seq'), may hold values from -0.078125 to 0.078125
- up_weight: bfloat16 [6144, 36864], P('head', 'seq'), may hold values from -0.078125 to 0.078125
- down_weight: bfloat16 [36864, 6144], P('seq', 'head'), may hold values from -0.0625 to 0.0625
Outputs:
- attention_out: bfloat16 [16384, 8192], P('seq', 'head')
- moe_out: bfloat16 [16384, 6144], P('seq', 'head')
Inputs may be any that keep to these rules, and one draw needn't show every extreme that they name: `expert_ids`: in each aligned block of 256 tokens, each expert named in placement is named by at most 8 tokens, and the same one of them by exactly 8 tokens in every block; the two ids of a token differ. `placement`: 4 different expert numbers, among them always 0 and 31. `log_decay`: every entry is negative.
All inputs are finite; a program needn't handle non-finite values.
Results may differ from a plain program's by a relative error of at most 0.0058.
Values may be sent and summed in bfloat16 or wider, within the bound.
No kernel may reach another device: no remote copies, remote signals or barrier semaphores. Data moves between devices by JAX's collectives and lax.ppermute only.
A program may use at most 64 MiB of HBM per device.

v0:
```python
import jax
import jax.numpy as jnp
from jax import lax
from jax.sharding import PartitionSpec as P

EXP_FLY = 4
CAP = 8


norm_eps = 1e-06


def prefix(part, axis, combine, identity):
    place = lax.axis_index(axis)
    gathered = jax.tree.map(lambda a: lax.all_gather(a, axis), part)
    state = jax.tree.map(lambda a, e: jnp.zeros_like(a) + jnp.asarray(e, a.dtype), part, identity)

    def one(step, state):
        return combine(
            state, jax.tree.map(lambda a: lax.dynamic_index_in_dim(a, step, 0, False), gathered)
        )

    return lax.fori_loop(0, place, one, state)


def slot_table(pairs, placement, slots):
    flat = pairs.reshape(-1)
    match = (flat[:, None] == placement[None, :]).astype(jnp.int32)
    rank = jnp.cumsum(match, axis=0) - 1
    order = jnp.arange(slots, dtype=jnp.int32)
    hits = (match[None, :, :] == 1) & (rank[None, :, :] == order[:, None, None])
    return jnp.transpose(hits, (2, 0, 1))


def combine_states(earlier, later):
    return (earlier[0] * later[0], later[0][:, None, None] * earlier[1] + later[1])


def per_device(
    queries,
    key_input,
    value_input,
    out_gate,
    log_decay,
    norm_gain,
    features,
    expert_ids,
    route_weight,
    placement,
    gate_weight,
    up_weight,
    down_weight,
):
    tokens = queries.shape[0]
    heads_here = log_decay.shape[0]
    width = queries.shape[1] // heads_here
    query_h = queries.reshape(tokens, heads_here, width)
    key_h = key_input.reshape(tokens, heads_here, width)
    value_h = value_input.reshape(tokens, heads_here, width)
    decay_sum = jnp.cumsum(log_decay, axis=1)
    last = decay_sum[:, -1]
    key_scaled = key_h.astype(jnp.float32) * jnp.exp(last[:, None] - decay_sum).T[:, :, None]
    local_state = jnp.einsum(
        "thd,the->hde", key_scaled, value_h.astype(jnp.float32), precision=lax.Precision.HIGHEST
    )
    ones = jnp.ones_like(last)
    zeros = jnp.zeros_like(local_state)
    moved = prefix((jnp.exp(last), local_state), "seq", combine_states, (ones, zeros))
    state_in = moved[1]
    scores = jnp.einsum("thd,shd->hts", query_h, key_h, preferred_element_type=jnp.float32)
    lower = jnp.arange(tokens)[:, None] >= jnp.arange(tokens)[None, :]
    spread = decay_sum[:, :, None] - decay_sum[:, None, :]
    weights = jnp.exp(jnp.where(lower[None], spread, -jnp.inf))
    probs = (scores * weights).astype(jnp.bfloat16)
    intra = jnp.einsum("hts,shd->thd", probs, value_h, preferred_element_type=jnp.float32)
    query_scaled = query_h.astype(jnp.float32) * jnp.exp(decay_sum).T[:, :, None]
    inter = jnp.einsum("thd,hde->the", query_scaled, state_in, precision=lax.Precision.HIGHEST)
    mixed = intra + inter
    power = jnp.mean(mixed * mixed, axis=-1, keepdims=True)
    normed = mixed * lax.rsqrt(power + norm_eps)
    gates = jax.nn.sigmoid(out_gate.reshape(tokens, heads_here, width).astype(jnp.float32))
    attention_out = (
        (normed * norm_gain.reshape(heads_here, width) * gates)
        .reshape(tokens, -1)
        .astype(jnp.bfloat16)
    )
    seq_count = lax.axis_size("seq")
    group = seq_count // EXP_FLY
    hits = slot_table(expert_ids, placement, CAP).reshape(EXP_FLY, CAP, tokens, 2)
    pick = jnp.sum(hits.astype(jnp.int32), axis=3).astype(jnp.bfloat16)
    share = jnp.sum(hits.astype(jnp.float32) * route_weight[None, None, :, :], axis=3)
    outgoing = jnp.einsum("jct,td->jcd", pick, features, preferred_element_type=jnp.float32).astype(
        jnp.bfloat16
    )
    fanned = jnp.broadcast_to(outgoing[:, None], (EXP_FLY, group) + outgoing.shape[1:]).reshape(
        seq_count, CAP, -1
    )
    arrived = lax.all_to_all(fanned, "seq", split_axis=0, concat_axis=0, tiled=True)
    slot_rows = arrived.reshape(seq_count * CAP, -1)
    gate = jnp.dot(slot_rows, gate_weight, preferred_element_type=jnp.float32)
    up = jnp.dot(slot_rows, up_weight, preferred_element_type=jnp.float32)
    gate_part, up_part = (
        lax.psum_scatter(gate, "head", scatter_dimension=0, tiled=True),
        lax.psum_scatter(up, "head", scatter_dimension=0, tiled=True),
    )
    hidden_part = (jax.nn.silu(gate_part) * up_part).astype(jnp.bfloat16)
    hidden = lax.all_gather(hidden_part, "head", axis=0, tiled=True)
    partial_value = jnp.dot(hidden, down_weight, preferred_element_type=jnp.float32).astype(
        jnp.bfloat16
    )
    returned = lax.all_to_all(
        partial_value.reshape(seq_count, CAP, -1), "seq", split_axis=0, concat_axis=0, tiled=True
    )
    expert_out = jnp.sum(returned.reshape(EXP_FLY, group, CAP, -1).astype(jnp.float32), axis=1)
    moe_out = jnp.einsum("jct,jcd->td", share, expert_out, precision=lax.Precision.HIGHEST).astype(
        jnp.bfloat16
    )
    return (attention_out, moe_out)


def solution(mesh):
    placed = (
        P("seq", "head"),
        P("seq", "head"),
        P("seq", "head"),
        P("seq", "head"),
        P("head", "seq"),
        P("head"),
        P("seq", "head"),
        P("seq", None),
        P("seq", None),
        P(),
        P("head", "seq"),
        P("head", "seq"),
        P("seq", "head"),
    )
    return jax.shard_map(
        per_device,
        mesh=mesh,
        in_specs=placed,
        out_specs=(P("seq", "head"), P("seq", "head")),
        check_vma=False,
    )
```

profile of v0, /device:TPU:993, one launch (start us, length us, event | category | flops | bytes accessed | tf_op | source)
XLA Modules:
  0.0 537.7 jit_solution(2306715893396669575)
XLA Ops:
  9.8 1.2 reduce-window.16
  13.0 65.3 %all_to_all.10 = bf16[64,8,384]{2,1,0:T(8,128)(2,1)S(1)} all-to-all(bf16[64,8,384]{2,1,0:T(8,128)(2,1)S(1)} %bitcast.99), channel_id=1, replica_groups=mesh['seq'=64,'head'=16] {'seq'}, dimensions={0} | all-to-all | bytes 786432 | tf_op jit(solution)/shard_map/all_to_all | solution.py:98
  78.3 1.6 fusion.18
  80.0 1.7 fusion.16
  81.8 1.2 reduce-window.14
  83.8 1.1 fusion.9
  85.0 91.9 %reduce-scatter.3.cloned.1.call-done = f32[32,576]{1,0:T(8,128)} async-done(((f32[512,576]{1,0:T(8,128)}), f32[32,576]{1,0:T(8,128)}) %reduce-scatter.3.cloned.1.call-update) | async-done | bytes 73744 | tf_op jit(solution)/shard_map/reduce_scatter | solution.py:103
  176.9 114.8 %reduce-scatter.5.cloned.1.call-done = f32[32,576]{1,0:T(8,128)} async-done(((f32[512,576]{1,0:T(8,128)}), f32[32,576]{1,0:T(8,128)}) %reduce-scatter.5.cloned.1.call-update) | async-done | bytes 73744 | tf_op jit(solution)/shard_map/reduce_scatter | solution.py:104
  292.6 17.7 %all_gather.16 = bf16[512,576]{1,0:T(8,128)(2,1)S(1)} all-gather(bf16[32,576]{1,0:T(8,128)(2,1)S(1)} %multiply_convert_fusion.1), channel_id=1, replica_groups=mesh['seq'=64,'head'=16] {'head'}, dimensions={0}, use_global_device_ids=true | all-gather | bytes 626688 | tf_op jit(solution)/shard_map/all_gather | solution.py:107
  310.3 1.3 fusion.2
  311.6 29.0 %all-to-all-start.1 = ((bf16[64,8,384]{2,1,0:T(8,128)(2,1)}), bf16[64,8,384]{2,1,0:T(8,128)(2,1)S(1)}, u32[]{:S(2)}, u32[]{:S(2)}) async-start(bf16[64,8,384]{2,1,0:T(8,128)(2,1)} %fusion.2), calls=%async_computation.3 | async-start | bytes 786432 | tf_op jit(solution)/shard_map/all_to_all | solution.py:111
  340.7 1.3 dynamic-slice
  342.7 113.5 %all-reduce = f32[256]{0:T(256)S(1)} all-reduce(f32[256]{0:T(256)S(1)} %bitcast_dynamic-update-slice_fusion), channel_id=2, replica_groups=mesh['seq'=64,'head'=16] {'seq'}, use_global_device_ids=true, to_apply=%add | all-reduce | flops 256 | bytes 2048
  456.8 1.2 fusion.3
  458.1 69.7 %while.12 = (s32[]{:T(128)}, f32[4,128,128]{2,1,0:T(8,128)S(1)}, s32[]{:T(128)}, f32[64,4]{1,0:T(8,128)S(1)}, f32[64,4,128,128]{3,2,1,0:T(8,128)}, /*index=5*/s32[]{:T(128)}, s32[]{:T(128)}, s32[]{:T(128)}) while((s32[]{:T(128)}, f32[4,128,128]{2,1,0:T(8,128)S(1)}, s32[]{:T(128)}, f32[64,4]{1,0:T(8,128)S(1)}, f32[64,4,128,128]{3,2,1,0:T(8,128)}, ...), condition=%wide.region_3.4_spmd, body=%wide.region_2.3_spmd.sunk | while | flops 131077 | bytes 786607 | solution.py:23
  458.1 1.1 bitcast_add_fusion.2
  459.3 1.1 bitcast_add_fusion.2
  461.5 1.1 bitcast_add_fusion.2
  463.7 1.1 bitcast_add_fusion.2
  465.9 1.1 bitcast_add_fusion.2
  468.1 1.1 bitcast_add_fusion.2
  470.3 1.1 bitcast_add_fusion.2
  472.5 1.1 bitcast_add_fusion.2
  474.7 1.1 bitcast_add_fusion.2
  (188 shorter events, 66.7 us)
Async XLA Ops:
  8.0 70.3 %copy-start = (bf16[384,576]{0,1:T(8,128)(2,1)S(1)}, bf16[384,576]{0,1:T(8,128)(2,1)}, u32[]{:S(2)}) copy-start(bf16[384,576]{0,1:T(8,128)(2,1)} %param.25) | copy-start | bytes 1327108
  8.0 4.8 copy-start.7
  8.0 168.9 %reduce-scatter.3.cloned.1.call-start = ((), (), s32[]{:S(2)}) async-start(), calls=%async_computation.4 | async-start | bytes 1392640 | tf_op jit(solution)/shard_map/reduce_scatter | solution.py:103
  78.3 1.7 copy-start.1
  80.0 1.8 copy-start.8
  80.0 3.6 copy-start.5
  80.0 211.7 %reduce-scatter.5.cloned.1.call-start = ((), (), s32[]{:S(2)}) async-start(), calls=%async_computation.5 | async-start | bytes 1392640 | tf_op jit(solution)/shard_map/reduce_scatter | solution.py:104
  81.7 2.1 copy-start.4
  81.7 228.6 %copy-start.2 = (bf16[576,384]{1,0:T(8,128)(2,1)S(1)}, bf16[576,384]{1,0:T(8,128)(2,1)}, u32[]{:S(2)}) copy-start(bf16[576,384]{1,0:T(8,128)(2,1)} %param.27) | copy-start | bytes 1327108
  81.7 376.3 %all-gather.4.cloned.1.call-start = ((), (), s32[]{:S(2)}) async-start(), calls=%async_computation.6 | async-start | bytes 17039360 | tf_op jit(solution)/shard_map/all_gather | solution.py:15
  310.3 146.0 %copy-start.3 = (bf16[256,512]{1,0:T(8,128)(2,1)S(1)}, bf16[256,512]{1,0:T(8,128)(2,1)}, u32[]{:S(2)}) copy-start(bf16[256,512]{1,0:T(8,128)(2,1)} %param.18) | copy-start | bytes 786436
  311.6 145.1 %copy-start.10 = (f32[256,2]{0,1:T(2,128)S(1)}, f32[256,2]{0,1:T(2,128)}, u32[]{:S(2)}) copy-start(f32[256,2]{0,1:T(2,128)} %param.23) | copy-start | bytes 6148
  311.6 145.1 %all-to-all-start.1 = ((bf16[64,8,384]{2,1,0:T(8,128)(2,1)}), bf16[64,8,384]{2,1,0:T(8,128)(2,1)S(1)}, u32[]{:S(2)}, u32[]{:S(2)}) async-start(bf16[64,8,384]{2,1,0:T(8,128)(2,1)} %fusion.2), calls=%async_computation.3 | async-start | bytes 786432 | tf_op jit(solution)/shard_map/all_to_all | solution.py:111
  458.1 69.7 %copy-start.6 = (bf16[256,512]{1,0:T(8,128)(2,1)S(1)}, bf16[256,512]{1,0:T(8,128)(2,1)}, u32[]{:S(2)}) copy-start(bf16[256,512]{1,0:T(8,128)(2,1)} %param.15) | copy-start | bytes 786436
  528.6 0.7 copy-start.9
Sparse Core Ops, SparseCore 0:
  80.1 96.7 reduce-scatter.2
  182.1 109.4 reduce-scatter.4
Sparse Core Ops, SparseCore 1:
  85.5 138.1 all-gather.3
where the time goes:
time: 540 us; the launch traced here: 538 us
  waiting for transfers between devices  207 us (38%)
  blocking collectives  196 us (36%)
  other arithmetic  72.7 us (13%)
  starting transfers between devices  29.2 us (5%)
  between operations  16.5 us (3%)
  matrix products  8.39 us (2%)
  local copies, waits for them, and re-layouts  5.59 us (1%)
    reduce_scatter x1, waiting for transfers between devices, per_device(): lax.psum_scatter(up, 'head', scatter_dimension=0, tiled=True)  115 us
    unnamed x1, blocking collectives  113 us
    reduce_scatter x1, waiting for transfers between devices, per_device(): lax.psum_scatter(gate, 'head', scatter_dimension=0, tiled=True)  91.9 us
    add x63, other arithmetic, combine_states(): later[0][:, None, None] * earlier[1] + later[1]  66.9 us
    all_to_all x1, blocking collectives, per_device(): lax.all_to_all(fanned, 'seq', split_axis=0, concat_axis=0, tiled=True)  65.3 us
    all_to_all x1, starting transfers between devices, per_device(): lax.all_to_all(partial_value.reshape(seq_count, CAP, -1), 'seq', split_ax...  29 us
    all_gather x1, blocking collectives, per_device(): hidden = lax.all_gather(hidden_part, 'head', axis=0, tiled=True)  17.7 us
  transfers between devices with their start and end apart: 4, of which 2 were waited for; matrix products, arithmetic and copies ran while one was open for 2% of the time, Pallas kernels for 0%

commit v1 on v0

v1 whole, which is shorter than its diff:
```python
import jax
import jax.numpy as jnp
from jax import lax
from jax.sharding import PartitionSpec as P

EXP_FLY = 4
CAP = 8


norm_eps = 1e-06


def slot_table(pairs, placement, slots):
    flat = pairs.reshape(-1)
    match = (flat[:, None] == placement[None, :]).astype(jnp.int32)
    rank = jnp.cumsum(match, axis=0) - 1
    order = jnp.arange(slots, dtype=jnp.int32)
    hits = (match[None, :, :] == 1) & (rank[None, :, :] == order[:, None, None])
    return jnp.transpose(hits, (2, 0, 1))


def split3(x):
    first = x.astype(jnp.bfloat16)
    rest = x - first.astype(jnp.float32)
    second = rest.astype(jnp.bfloat16)
    third = (rest - second.astype(jnp.float32)).astype(jnp.bfloat16)
    return jnp.stack([first, second, third], axis=-1)


def per_device(
    queries,
    key_input,
    value_input,
    out_gate,
    log_decay,
    norm_gain,
    features,
    expert_ids,
    route_weight,
    placement,
    gate_weight,
    up_weight,
    down_weight,
):
    seq_count = lax.axis_size("seq")
    head_count = lax.axis_size("head")
    group = seq_count // EXP_FLY
    tokens = queries.shape[0]
    heads_here = log_decay.shape[0]
    width = queries.shape[1] // heads_here
    feat = features.shape[1]
    ff = gate_weight.shape[1]
    half_cap = CAP // 2
    row_len = half_cap * feat
    query_h = queries.reshape(tokens, heads_here, width)
    key_h = key_input.reshape(tokens, heads_here, width)
    value_h = value_input.reshape(tokens, heads_here, width)

    decay_sum = jnp.cumsum(log_decay, axis=1)
    last = decay_sum[:, -1]
    key_scaled = key_h.astype(jnp.float32) * jnp.exp(last[:, None] - decay_sum).T[:, :, None]
    local_state = jnp.einsum(
        "thd,the->hde", key_scaled, value_h.astype(jnp.float32), precision=lax.Precision.HIGHEST
    )
    state_piece = local_state.astype(jnp.bfloat16).reshape(seq_count, -1)
    piece_len = state_piece.shape[1]
    log_piece = jnp.repeat(split3(last), seq_count // heads_here, axis=0)
    log_piece = jnp.pad(log_piece, ((0, 0), (0, 125)))

    hits = slot_table(expert_ids, placement, CAP).reshape(EXP_FLY, CAP, tokens, 2)
    pick = jnp.sum(hits.astype(jnp.int32), axis=3).astype(jnp.bfloat16)
    share = jnp.sum(hits.astype(jnp.float32) * route_weight[None, None, :, :], axis=3)
    outgoing = jnp.einsum("jct,td->jcd", pick, features, preferred_element_type=jnp.float32).astype(
        jnp.bfloat16
    )
    fanned = jnp.broadcast_to(
        outgoing.reshape(EXP_FLY, 1, 2, row_len), (EXP_FLY, group // 2, 2, row_len)
    ).reshape(seq_count, row_len)

    arrived = lax.all_to_all(
        jnp.concatenate([fanned, state_piece, log_piece], axis=1),
        "seq",
        split_axis=0,
        concat_axis=0,
        tiled=True,
    )
    swap = [(i, i ^ 1) for i in range(seq_count)]
    own_rows = arrived[:, :row_len].reshape(seq_count * half_cap, feat)
    other_rows = lax.ppermute(own_rows, "seq", swap)

    logs = jnp.sum(
        arrived[:, row_len + piece_len : row_len + piece_len + 3].astype(jnp.float32), axis=1
    )
    at = jnp.arange(seq_count)
    later = jnp.where(at[None, :] > at[:, None], logs[None, :], 0.0)
    before = (at[None, :] < at[:, None]).astype(jnp.float32)
    spans = jnp.einsum("bu,cu->bc", before, later, precision=lax.Precision.HIGHEST)
    mix = jnp.where(at[None, :] < at[:, None], jnp.exp(spans), 0.0)
    pieces_in = arrived[:, row_len : row_len + piece_len].astype(jnp.float32)
    prefix_piece = jnp.dot(mix, pieces_in, precision=lax.Precision.HIGHEST).astype(jnp.bfloat16)

    slot_rows = jnp.concatenate([own_rows, other_rows], axis=0)
    both_weight = jnp.concatenate([gate_weight, up_weight], axis=1)
    gate_up = jnp.dot(slot_rows, both_weight, preferred_element_type=jnp.float32).astype(
        jnp.bfloat16
    )
    rows = slot_rows.shape[0]
    parts = lax.all_to_all(
        gate_up.reshape(head_count, rows // head_count, 2 * ff),
        "head",
        split_axis=0,
        concat_axis=0,
        tiled=True,
    )
    summed = jnp.sum(parts.astype(jnp.float32), axis=0)
    hidden_part = (jax.nn.silu(summed[:, :ff]) * summed[:, ff:]).astype(jnp.bfloat16)
    hidden = lax.all_to_all(
        jnp.broadcast_to(hidden_part[None], (head_count,) + hidden_part.shape),
        "head",
        split_axis=0,
        concat_axis=0,
        tiled=True,
    ).reshape(rows, ff)
    partial_value = jnp.dot(hidden, down_weight, preferred_element_type=jnp.float32).astype(
        jnp.bfloat16
    )
    pair = lax.ppermute(partial_value[rows // 2 :], "seq", swap)
    piece = (partial_value[: rows // 2].astype(jnp.float32) + pair.astype(jnp.float32)).astype(
        jnp.bfloat16
    )
    returned = lax.all_to_all(
        jnp.concatenate([piece.reshape(seq_count, row_len), prefix_piece], axis=1),
        "seq",
        split_axis=0,
        concat_axis=0,
        tiled=True,
    )
    expert_out = jnp.sum(
        returned[:, :row_len].reshape(EXP_FLY, group // 2, CAP, feat).astype(jnp.float32), axis=1
    )
    moe_out = jnp.einsum("jct,jcd->td", share, expert_out, precision=lax.Precision.HIGHEST).astype(
        jnp.bfloat16
    )
    state_in = returned[:, row_len:].reshape(heads_here, width, width).astype(jnp.float32)

    scores = jnp.einsum("thd,shd->hts", query_h, key_h, preferred_element_type=jnp.float32)
    lower = jnp.arange(tokens)[:, None] >= jnp.arange(tokens)[None, :]
    spread = decay_sum[:, :, None] - decay_sum[:, None, :]
    weights = jnp.exp(jnp.where(lower[None], spread, -jnp.inf))
    probs = (scores * weights).astype(jnp.bfloat16)
    intra = jnp.einsum("hts,shd->thd", probs, value_h, preferred_element_type=jnp.float32)
    query_scaled = query_h.astype(jnp.float32) * jnp.exp(decay_sum).T[:, :, None]
    inter = jnp.einsum("thd,hde->the", query_scaled, state_in, precision=lax.Precision.HIGHEST)
    mixed = intra + inter
    power = jnp.mean(mixed * mixed, axis=-1, keepdims=True)
    normed = mixed * lax.rsqrt(power + norm_eps)
    gates = jax.nn.sigmoid(out_gate.reshape(tokens, heads_here, width).astype(jnp.float32))
    attention_out = (
        (normed * norm_gain.reshape(heads_here, width) * gates)
        .reshape(tokens, -1)
        .astype(jnp.bfloat16)
    )
    return (attention_out, moe_out)


def solution(mesh):
    placed = (
        P("seq", "head"),
        P("seq", "head"),
        P("seq", "head"),
        P("seq", "head"),
        P("head", "seq"),
        P("head"),
        P("seq", "head"),
        P("seq", None),
        P("seq", None),
        P(),
        P("head", "seq"),
        P("head", "seq"),
        P("seq", "head"),
    )
    return jax.shard_map(
        per_device,
        mesh=mesh,
        in_specs=placed,
        out_specs=(P("seq", "head"), P("seq", "head")),
        check_vma=False,
    )
```

time: 540 us -> 204 us (0.38)
  the two profiles are of different devices: /device:TPU:993 before, /device:TPU:1 now
where the time goes in v1:
time: 204 us; the launch traced here: 203 us
  blocking collectives  105 us (51%)
  waiting for transfers between devices  59.4 us (29%)
  starting transfers between devices  15.8 us (8%)
  local copies, waits for them, and re-layouts  9.92 us (5%)
  other arithmetic  7.04 us (3%)
  matrix products  4.67 us (2%)
    all_to_all x1, blocking collectives, per_device(): lax.all_to_all(jnp.concatenate([fanned, state_piece, log_piece], axis=1),...  80.8 us
    all_to_all x1, waiting for transfers between devices, per_device(): lax.all_to_all(jnp.concatenate([piece.reshape(seq_count, row_len), prefix...  46.3 us
    all_to_all x1, blocking collectives, per_device(): lax.all_to_all(gate_up.reshape(head_count, rows // head_count, 2 * ff), '...  24.6 us
    all_to_all x1, waiting for transfers between devices, per_device(): lax.all_to_all(jnp.broadcast_to(hidden_part[None], (head_count,) + hidden...  11.3 us
    all_to_all x1, starting transfers between devices, per_device(): lax.all_to_all(jnp.concatenate([piece.reshape(seq_count, row_len), prefix...  4.56 us
    unnamed x28, local copies, waits for them, and re-layouts  4.56 us
    ppermute x1, starting transfers between devices, per_device(): pair = lax.ppermute(partial_value[rows // 2:], 'seq', swap)  4.18 us
  transfers between devices with their start and end apart: 4, of which 4 were waited for; matrix products, arithmetic and copies ran while one was open for 0% of the time, Pallas kernels for 0%

profile of v1, /device:TPU:1, one launch (start us, length us, event | category | flops | bytes accessed | tf_op | source)
XLA Modules:
  0.0 203.3 jit_solution(18228617643289176993)
XLA Ops:
  0.7 0.9 copy.89
  1.7 0.7 compare_convert_fusion.1
  2.4 1.2 reduce-window.16
  4.0 0.8 fusion.44
  4.8 0.7 reshape.185
  5.5 1.2 reduce-window.14
  7.4 1.1 copy.107
  10.6 0.8 reduce.2
  11.8 80.8 %all_to_all.34 = bf16[64,2,1344]{2,1,0:T(2,128)(2,1)S(1)} all-to-all(bf16[64,2,1344]{2,1,0:T(2,128)(2,1)S(1)} %reshape.205), channel_id=1, replica_groups=mesh['seq'=64,'head'=16] {'seq'}, dimensions={0} | all-to-all | bytes 688128 | tf_op jit(solution)/shard_map/all_to_all | solution.py:80
  93.3 3.4 %collective-permute-start = (bf16[256,384]{1,0:T(8,128)(2,1)S(1)}, bf16[256,384]{1,0:T(8,128)(2,1)S(1)}, u32[]{:S(2)}, u32[]{:S(2)}) collective-permute-start(bf16[256,384]{1,0:T(8,128)(2,1)S(1)} %reshape.194), channel_id=1, source_target_pairs={{0,16},{16,0},{32,48},{48,32},{64,80},{80,64},{96,112},{112,96},{1... | collective-permute-start | bytes 589832 | tf_op jit(solution)/shard_map/ppermute | solution.py:89
  96.7 1.0 collective-permute-done
  97.8 0.8 convolution_convert_fusion
  98.6 24.6 %all_to_all.35 = bf16[16,32,1152]{2,1,0:T(8,128)(2,1)S(1)} all-to-all(bf16[16,32,1152]{2,1,0:T(8,128)(2,1)S(1)} %bitcast.93), channel_id=1, replica_groups=mesh['seq'=64,'head'=16] {'head'}, dimensions={0} | all-to-all | bytes 2359296 | tf_op jit(solution)/shard_map/all_to_all | solution.py:108
  123.5 0.9 broadcast_in_dim.35
  124.4 3.6 %all-to-all-start.2 = ((bf16[16,32,576]{2,1,0:T(8,128)(2,1)}), bf16[16,32,576]{2,1,0:T(8,128)(2,1)S(1)}, u32[]{:S(2)}, u32[]{:S(2)}) async-start(bf16[16,32,576]{2,1,0:T(8,128)(2,1)} %broadcast_in_dim.35), calls=%async_computation.2 | async-start | bytes 1310720 | tf_op jit(solution)/shard_map/all_to_all | solution.py:117
  128.3 11.3 %all-to-all-done.2 = bf16[16,32,576]{2,1,0:T(8,128)(2,1)S(1)} async-done(((bf16[16,32,576]{2,1,0:T(8,128)(2,1)}), bf16[16,32,576]{2,1,0:T(8,128)(2,1)S(1)}, u32[]{:S(2)}, u32[]{:S(2)}) %all-to-all-start.2) | async-done | bytes 589856 | tf_op jit(solution)/shard_map/all_to_all | solution.py:117
  140.1 4.2 %collective-permute-start.1 = (bf16[256,384]{1,0:T(8,128)(2,1)S(1)}, bf16[256,384]{1,0:T(8,128)(2,1)S(1)}, u32[]{:S(2)}, u32[]{:S(2)}) collective-permute-start(bf16[256,384]{1,0:T(8,128)(2,1)S(1)} %slice.63), channel_id=1, source_target_pairs={{0,16},{16,0},{32,48},{48,32},{64,80},{80,64},{96,112},{112,96},{1... | collective-permute-start | bytes 589832 | tf_op jit(solution)/shard_map/ppermute | solution.py:127
  144.6 0.8 collective-permute-done.1
  145.6 0.9 reduce.3
  146.5 0.8 reshape.207
  147.3 4.6 %all-to-all-start.3 = ((bf16[64,2,1280]{2,1,0:T(2,128)(2,1)}), bf16[64,2,1280]{2,1,0:T(2,128)(2,1)S(1)}, u32[]{:S(2)}, u32[]{:S(2)}) async-start(bf16[64,2,1280]{2,1,0:T(2,128)(2,1)} %reshape.207), calls=%async_computation.3 | async-start | bytes 655360 | tf_op jit(solution)/shard_map/all_to_all | solution.py:131
  152.3 46.3 %all-to-all-done.3 = bf16[64,2,1280]{2,1,0:T(2,128)(2,1)S(1)} async-done(((bf16[64,2,1280]{2,1,0:T(2,128)(2,1)}), bf16[64,2,1280]{2,1,0:T(2,128)(2,1)S(1)}, u32[]{:S(2)}, u32[]{:S(2)}) %all-to-all-start.3) | async-done | bytes 327712 | tf_op jit(solution)/shard_map/all_to_all | solution.py:131
  201.2 0.8 copy.102
  202.0 1.2 fusion.2
  (79 shorter events, 8.8 us)
Async XLA Ops:
  0.6 138.9 %copy-start = (bf16[576,384]{1,0:T(8,128)(2,1)S(1)}, bf16[576,384]{1,0:T(8,128)(2,1)}, u32[]{:S(2)}) copy-start(bf16[576,384]{1,0:T(8,128)(2,1)} %param.25) | copy-start | bytes 1327108
  0.6 7.9 %copy-start.8 = (bf16[256,512]{1,0:T(8,128)(2,1)S(1)}, bf16[256,512]{1,0:T(8,128)(2,1)}, u32[]{:S(2)}) copy-start(bf16[256,512]{1,0:T(8,128)(2,1)} %param.15) | copy-start | bytes 786436
  7.4 2.2 %copy-start.3 = (bf16[256,384]{1,0:T(8,128)(2,1)S(1)}, bf16[256,384]{1,0:T(8,128)(2,1)}, u32[]{:S(2)}) copy-start(bf16[256,384]{1,0:T(8,128)(2,1)} %param.19) | copy-start | bytes 589828
  92.6 5.2 %copy-start.6 = (bf16[384,576]{0,1:T(8,128)(2,1)S(1)}, bf16[384,576]{0,1:T(8,128)(2,1)}, u32[]{:S(2)}) copy-start(bf16[384,576]{0,1:T(8,128)(2,1)} %param.24) | copy-start | bytes 1327108
  92.6 5.2 %copy-start.7 = (bf16[384,576]{0,1:T(8,128)(2,1)S(1)}, bf16[384,576]{0,1:T(8,128)(2,1)}, u32[]{:S(2)}) copy-start(bf16[384,576]{0,1:T(8,128)(2,1)} %param.23) | copy-start | bytes 1327108
  93.3 4.5 %collective-permute-start = (bf16[256,384]{1,0:T(8,128)(2,1)S(1)}, bf16[256,384]{1,0:T(8,128)(2,1)S(1)}, u32[]{:S(2)}, u32[]{:S(2)}) collective-permute-start(bf16[256,384]{1,0:T(8,128)(2,1)S(1)} %reshape.194), channel_id=1, source_target_pairs={{0,16},{16,0},{32,48},{48,32},{64,80},{80,64},{96,112},{112,96},{1... | collective-permute-start | bytes 589832 | tf_op jit(solution)/shard_map/ppermute | solution.py:89
  124.4 15.2 %all-to-all-start.2 = ((bf16[16,32,576]{2,1,0:T(8,128)(2,1)}), bf16[16,32,576]{2,1,0:T(8,128)(2,1)S(1)}, u32[]{:S(2)}, u32[]{:S(2)}) async-start(bf16[16,32,576]{2,1,0:T(8,128)(2,1)} %broadcast_in_dim.35), calls=%async_computation.2 | async-start | bytes 1310720 | tf_op jit(solution)/shard_map/all_to_all | solution.py:117
  140.1 5.2 %collective-permute-start.1 = (bf16[256,384]{1,0:T(8,128)(2,1)S(1)}, bf16[256,384]{1,0:T(8,128)(2,1)S(1)}, u32[]{:S(2)}, u32[]{:S(2)}) collective-permute-start(bf16[256,384]{1,0:T(8,128)(2,1)S(1)} %slice.63), channel_id=1, source_target_pairs={{0,16},{16,0},{32,48},{48,32},{64,80},{80,64},{96,112},{112,96},{1... | collective-permute-start | bytes 589832 | tf_op jit(solution)/shard_map/ppermute | solution.py:127
  145.5 6.3 %copy-start.1 = (bf16[256,512]{1,0:T(8,128)(2,1)S(1)}, bf16[256,512]{1,0:T(8,128)(2,1)}, u32[]{:S(2)}) copy-start(bf16[256,512]{1,0:T(8,128)(2,1)} %param.16) | copy-start | bytes 786436
  147.3 5.0 %copy-start.5 = (f32[256,2]{0,1:T(2,128)S(1)}, f32[256,2]{0,1:T(2,128)}, u32[]{:S(2)}) copy-start(f32[256,2]{0,1:T(2,128)} %param.21) | copy-start | bytes 6148
  147.3 51.3 %all-to-all-start.3 = ((bf16[64,2,1280]{2,1,0:T(2,128)(2,1)}), bf16[64,2,1280]{2,1,0:T(2,128)(2,1)S(1)}, u32[]{:S(2)}, u32[]{:S(2)}) async-start(bf16[64,2,1280]{2,1,0:T(2,128)(2,1)} %reshape.207), calls=%async_computation.3 | async-start | bytes 655360 | tf_op jit(solution)/shard_map/all_to_all | solution.py:131
  198.8 1.0 copy-start.2
  200.4 0.7 copy-start.4

commit v2 on v1

--- a/solution.py
+++ b/solution.py
@@ -66,6 +66,10 @@
     piece_len = state_piece.shape[1]
     log_piece = jnp.repeat(split3(last), seq_count // heads_here, axis=0)
     log_piece = jnp.pad(log_piece, ((0, 0), (0, 125)))
+    swap = [(i, i ^ 1) for i in range(seq_count)]
+    other_gate = lax.ppermute(gate_weight, "seq", swap)
+    other_up = lax.ppermute(up_weight, "seq", swap)
+    other_down = lax.ppermute(down_weight, "seq", swap)
 
     hits = slot_table(expert_ids, placement, CAP).reshape(EXP_FLY, CAP, tokens, 2)
     pick = jnp.sum(hits.astype(jnp.int32), axis=3).astype(jnp.bfloat16)
@@ -84,50 +88,45 @@
         concat_axis=0,
         tiled=True,
     )
-    swap = [(i, i ^ 1) for i in range(seq_count)]
-    own_rows = arrived[:, :row_len].reshape(seq_count * half_cap, feat)
-    other_rows = lax.ppermute(own_rows, "seq", swap)
+    slot_rows = arrived[:, :row_len].reshape(seq_count * half_cap, feat)
+    arrived = arrived[:, row_len:]
 
-    logs = jnp.sum(
-        arrived[:, row_len + piece_len : row_len + piece_len + 3].astype(jnp.float32), axis=1
-    )
+    logs = jnp.sum(arrived[:, piece_len : piece_len + 3].astype(jnp.float32), axis=1)
     at = jnp.arange(seq_count)
     later = jnp.where(at[None, :] > at[:, None], logs[None, :], 0.0)
     before = (at[None, :] < at[:, None]).astype(jnp.float32)
     spans = jnp.einsum("bu,cu->bc", before, later, precision=lax.Precision.HIGHEST)
     mix = jnp.where(at[None, :] < at[:, None], jnp.exp(spans), 0.0)
-    pieces_in = arrived[:, row_len : row_len + piece_len].astype(jnp.float32)
-    prefix_piece = jnp.dot(mix, pieces_in, precision=lax.Precision.HIGHEST).astype(jnp.bfloat16)
-
-    slot_rows = jnp.concatenate([own_rows, other_rows], axis=0)
-    both_weight = jnp.concatenate([gate_weight, up_weight], axis=1)
+    pieces_in = arrived[:, :piece_len].astype(jnp.float32)
+    prefix_piece = jnp.dot(mix, pieces_in, precision=lax.Precision.HIGHEST).astype(
+        jnp.bfloat16
+    )
+    both_weight = jnp.concatenate([gate_weight, other_gate, up_weight, other_up], axis=1)
     gate_up = jnp.dot(slot_rows, both_weight, preferred_element_type=jnp.float32).astype(
         jnp.bfloat16
     )
     rows = slot_rows.shape[0]
     parts = lax.all_to_all(
-        gate_up.reshape(head_count, rows // head_count, 2 * ff),
+        gate_up.reshape(head_count, rows // head_count, 4 * ff),
         "head",
         split_axis=0,
         concat_axis=0,
         tiled=True,
     )
     summed = jnp.sum(parts.astype(jnp.float32), axis=0)
-    hidden_part = (jax.nn.silu(summed[:, :ff]) * summed[:, ff:]).astype(jnp.bfloat16)
+    hidden_part = (jax.nn.silu(summed[:, : 2 * ff]) * summed[:, 2 * ff :]).astype(jnp.bfloat16)
     hidden = lax.all_to_all(
         jnp.broadcast_to(hidden_part[None], (head_count,) + hidden_part.shape),
         "head",
         split_axis=0,
         concat_axis=0,
         tiled=True,
-    ).reshape(rows, ff)
-    partial_value = jnp.dot(hidden, down_weight, preferred_element_type=jnp.float32).astype(
-        jnp.bfloat16
-    )
-    pair = lax.ppermute(partial_value[rows // 2 :], "seq", swap)
-    piece = (partial_value[: rows // 2].astype(jnp.float32) + pair.astype(jnp.float32)).astype(
-        jnp.bfloat16
-    )
+    ).reshape(rows, 2 * ff)
+    piece = jnp.dot(
+        hidden,
+        jnp.concatenate([down_weight, other_down], axis=0),
+        preferred_element_type=jnp.float32,
+    ).astype(jnp.bfloat16)
     returned = lax.all_to_all(
         jnp.concatenate([piece.reshape(seq_count, row_len), prefix_piece], axis=1),
         "seq",
@@ -179,6 +178,7 @@
         P("head", "seq"),
         P("seq", "head"),
     )
+
     return jax.shard_map(
         per_device,
         mesh=mesh,

time: 204 us -> 200 us (0.980)
  blocking collectives: 105 us -> 0 us
  waiting for transfers between devices: 59.4 us -> 115 us
  starting transfers between devices: 15.8 us -> 59.3 us
  matrix products: 4.67 us -> 6.77 us
    all_to_all x2 -> x0, blocking collectives: 105 us -> none  [the longest x1 80.8 us: per_device(): lax.all_to_all(jnp.concatenate([fanned, state_piece, log_piece], axis=1),...]
    all_to_all x0 -> x2, waiting for transfers between devices: none -> 59.1 us  [the longest x1 46.2 us: per_device(): lax.all_to_all(jnp.concatenate([fanned, state_piece, log_piece], axis=1),...]
    all_to_all x0 -> x2, starting transfers between devices: none -> 37.3 us  [the longest x1 30.4 us: per_device(): lax.all_to_all(jnp.concatenate([fanned, state_piece, log_piece], axis=1),...]
    all_to_all x1, starting transfers between devices: 4.56 us -> 9.15 us  [per_device(): lax.all_to_all(jnp.concatenate([piece.reshape(seq_count, row_len), prefix...]
    dot_general x1, matrix products: 0.82 us -> 2.97 us  [per_device(): jnp.dot(slot_rows, both_weight, preferred_element_type=jnp.float32)]
    ppermute x2 -> x3, starting transfers between devices: 7.63 us -> 8.05 us  [the longest x1 3.72 us: per_device(): other_down = lax.ppermute(down_weight, 'seq', swap)]
    unnamed x28 -> x30, local copies, waits for them, and re-layouts: 4.56 us -> 4.86 us
  transfers between devices with their start and end apart: 4 -> 7, of which waited for: 4 -> 4; matrix products, arithmetic and copies ran while one was open for 0% -> 1% of each run, Pallas kernels for 0% -> 0%
where the time goes in v2:
time: 200 us
  waiting for transfers between devices  115 us (58%)
  starting transfers between devices  59.3 us (30%)
  local copies, waits for them, and re-layouts  10.2 us (5%)
  other arithmetic  6.92 us (3%)
  matrix products  6.77 us (3%)
    all_to_all x1, waiting for transfers between devices, per_device(): lax.all_to_all(jnp.concatenate([piece.reshape(seq_count, row_len), prefix...  46.2 us
    all_to_all x1, waiting for transfers between devices, per_device(): lax.all_to_all(jnp.concatenate([fanned, state_piece, log_piece], axis=1),...  46.2 us
    all_to_all x1, starting transfers between devices, per_device(): lax.all_to_all(jnp.concatenate([fanned, state_piece, log_piece], axis=1),...  30.4 us
    all_to_all x1, waiting for transfers between devices, per_device(): lax.all_to_all(gate_up.reshape(head_count, rows // head_count, 4 * ff), '...  12.8 us
    all_to_all x1, waiting for transfers between devices, per_device(): lax.all_to_all(jnp.broadcast_to(hidden_part[None], (head_count,) + hidden...  9.91 us
    all_to_all x1, starting transfers between devices, per_device(): lax.all_to_all(jnp.concatenate([piece.reshape(seq_count, row_len), prefix...  9.15 us
    all_to_all x1, starting transfers between devices, per_device(): lax.all_to_all(gate_up.reshape(head_count, rows // head_count, 4 * ff), '...  6.89 us
    unnamed x30, local copies, waits for them, and re-layouts  4.86 us
  transfers between devices with their start and end apart: 7, of which 4 were waited for; matrix products, arithmetic and copies ran while one was open for 1% of the time, Pallas kernels for 0%

profile of v2, /device:TPU:1, one launch (start us, length us, event | category | flops | bytes accessed | tf_op | source)
XLA Modules:
  0.0 199.5 jit_solution(13507082582583640040)
XLA Ops:
  0.7 0.9 copy.89
  2.4 1.2 reduce-window.16
  4.0 0.8 fusion.48
  5.5 1.2 reduce-window.14
  7.4 1.1 copy.107
  10.6 0.8 reduce.2
  11.5 1.1 reshape.205
  12.6 30.4 %all-to-all-start = ((bf16[64,2,1344]{2,1,0:T(2,128)(2,1)}), bf16[64,2,1344]{2,1,0:T(2,128)(2,1)S(1)}, u32[]{:S(2)}, u32[]{:S(2)}) async-start(bf16[64,2,1344]{2,1,0:T(2,128)(2,1)} %reshape.205), calls=%async_computation | async-start | bytes 720896 | tf_op jit(solution)/shard_map/all_to_all | solution.py:84
  43.0 2.4 %collective-permute-start = (bf16[384,576]{0,1:T(8,128)(2,1)S(1)}, bf16[384,576]{0,1:T(8,128)(2,1)}, u32[]{:S(2)}, u32[]{:S(2)}) collective-permute-start(bf16[384,576]{0,1:T(8,128)(2,1)S(1)} %copy-done.6), channel_id=1, source_target_pairs={{0,16},{16,0},{32,48},{48,32},{64,80},{80,64},{96,112},{112,96},{1... | collective-permute-start | bytes 1327112 | tf_op jit(solution)/shard_map/ppermute | solution.py:70
  45.4 2.0 collective-permute-start.1
  47.3 46.2 %all-to-all-done = bf16[64,2,1344]{2,1,0:T(2,128)(2,1)S(1)} async-done(((bf16[64,2,1344]{2,1,0:T(2,128)(2,1)}), bf16[64,2,1344]{2,1,0:T(2,128)(2,1)S(1)}, u32[]{:S(2)}, u32[]{:S(2)}) %all-to-all-start) | async-done | bytes 344096 | tf_op jit(solution)/shard_map/all_to_all | solution.py:84
  94.2 3.0 %convolution_convert_fusion = bf16[256,2304]{1,0:T(8,128)(2,1)} fusion(bf16[256,384]{1,0:T(8,128)(2,1)S(1)} %reshape.194, bf16[384,576]{0,1:T(8,128)(2,1)} %collective-permute-done.1, bf16[384,576]{0,1:T(8,128)(2,1)S(1)} %copy-done.5, bf16[384,576]{0,1:T(8,128)(2,1)} %collective-permute-done, bf16[384,576]{0,1:T(8,128)(2,1)S(1)} %copy-done.6), kind=kOutput, calls=%fused_computation | convolution fusion | flops 460652544 | bytes 3145728 | tf_op jit(solution)/shard_map/dot_general | solution.py:105
  97.2 6.9 %all-to-all-start.1 = ((bf16[16,16,2304]{2,1,0:T(8,128)(2,1)}), bf16[16,16,2304]{2,1,0:T(8,128)(2,1)S(1)}, u32[]{:S(2)}, u32[]{:S(2)}) async-start(bf16[16,16,2304]{2,1,0:T(8,128)(2,1)} %bitcast.9), calls=%async_computation.1 | async-start | bytes 2359296 | tf_op jit(solution)/shard_map/all_to_all | solution.py:109
  104.1 3.7 %collective-permute-start.2 = (bf16[576,384]{1,0:T(8,128)(2,1)S(1)}, bf16[576,384]{1,0:T(8,128)(2,1)S(1)}, u32[]{:S(2)}, u32[]{:S(2)}) collective-permute-start(bf16[576,384]{1,0:T(8,128)(2,1)S(1)} %copy-done.7), channel_id=1, source_target_pairs={{0,16},{16,0},{32,48},{48,32},{64,80},{80,64},{96,112},{112,96},{1... | collective-permute-start | bytes 1327112 | tf_op jit(solution)/shard_map/ppermute | solution.py:72
  107.9 12.8 %all-to-all-done.1 = bf16[16,16,2304]{2,1,0:T(8,128)(2,1)S(1)} async-done(((bf16[16,16,2304]{2,1,0:T(8,128)(2,1)}), bf16[16,16,2304]{2,1,0:T(8,128)(2,1)S(1)}, u32[]{:S(2)}, u32[]{:S(2)}) %all-to-all-start.1) | async-done | bytes 1179680 | tf_op jit(solution)/shard_map/all_to_all | solution.py:109
  120.9 0.9 broadcast_in_dim.35
  121.8 4.8 %all-to-all-start.2 = ((bf16[16,16,1152]{2,1,0:T(8,128)(2,1)}), bf16[16,16,1152]{2,1,0:T(8,128)(2,1)S(1)}, u32[]{:S(2)}, u32[]{:S(2)}) async-start(bf16[16,16,1152]{2,1,0:T(8,128)(2,1)} %broadcast_in_dim.35), calls=%async_computation.2 | async-start | bytes 1179648 | tf_op jit(solution)/shard_map/all_to_all | solution.py:118
  127.1 9.9 %all-to-all-done.2 = bf16[16,16,1152]{2,1,0:T(8,128)(2,1)S(1)} async-done(((bf16[16,16,1152]{2,1,0:T(8,128)(2,1)}), bf16[16,16,1152]{2,1,0:T(8,128)(2,1)S(1)}, u32[]{:S(2)}, u32[]{:S(2)}) %all-to-all-start.2) | async-done | bytes 589856 | tf_op jit(solution)/shard_map/all_to_all | solution.py:118
  137.7 0.9 reduce.3
  138.6 0.8 reshape.207
  139.4 9.2 %all-to-all-start.3 = ((bf16[64,2,1280]{2,1,0:T(2,128)(2,1)}), bf16[64,2,1280]{2,1,0:T(2,128)(2,1)S(1)}, u32[]{:S(2)}, u32[]{:S(2)}) async-start(bf16[64,2,1280]{2,1,0:T(2,128)(2,1)} %reshape.207), calls=%async_computation.3 | async-start | bytes 655360 | tf_op jit(solution)/shard_map/all_to_all | solution.py:130
  149.0 46.2 %all-to-all-done.3 = bf16[64,2,1280]{2,1,0:T(2,128)(2,1)S(1)} async-done(((bf16[64,2,1280]{2,1,0:T(2,128)(2,1)}), bf16[64,2,1280]{2,1,0:T(2,128)(2,1)S(1)}, u32[]{:S(2)}, u32[]{:S(2)}) %all-to-all-start.3) | async-done | bytes 327712 | tf_op jit(solution)/shard_map/all_to_all | solution.py:130
  197.3 0.8 copy.102
  198.3 1.2 fusion.9
  (83 shorter events, 9.2 us)
Async XLA Ops:
  0.6 195.0 %copy-start = (bf16[256,512]{1,0:T(8,128)(2,1)S(1)}, bf16[256,512]{1,0:T(8,128)(2,1)}, u32[]{:S(2)}) copy-start(bf16[256,512]{1,0:T(8,128)(2,1)} %param.13) | copy-start | bytes 786436
  0.6 7.9 %copy-start.8 = (bf16[256,512]{1,0:T(8,128)(2,1)S(1)}, bf16[256,512]{1,0:T(8,128)(2,1)}, u32[]{:S(2)}) copy-start(bf16[256,512]{1,0:T(8,128)(2,1)} %param.15) | copy-start | bytes 786436
  7.4 2.2 %copy-start.2 = (bf16[256,384]{1,0:T(8,128)(2,1)S(1)}, bf16[256,384]{1,0:T(8,128)(2,1)}, u32[]{:S(2)}) copy-start(bf16[256,384]{1,0:T(8,128)(2,1)} %param.19) | copy-start | bytes 589828
  10.1 32.9 %copy-start.6 = (bf16[384,576]{0,1:T(8,128)(2,1)S(1)}, bf16[384,576]{0,1:T(8,128)(2,1)}, u32[]{:S(2)}) copy-start(bf16[384,576]{0,1:T(8,128)(2,1)} %param.23) | copy-start | bytes 1327108
  10.1 35.2 %copy-start.5 = (bf16[384,576]{0,1:T(8,128)(2,1)S(1)}, bf16[384,576]{0,1:T(8,128)(2,1)}, u32[]{:S(2)}) copy-start(bf16[384,576]{0,1:T(8,128)(2,1)} %param.24) | copy-start | bytes 1327108
  12.6 81.0 %all-to-all-start = ((bf16[64,2,1344]{2,1,0:T(2,128)(2,1)}), bf16[64,2,1344]{2,1,0:T(2,128)(2,1)S(1)}, u32[]{:S(2)}, u32[]{:S(2)}) async-start(bf16[64,2,1344]{2,1,0:T(2,128)(2,1)} %reshape.205), calls=%async_computation | async-start | bytes 720896 | tf_op jit(solution)/shard_map/all_to_all | solution.py:84
  43.0 51.2 %collective-permute-start = (bf16[384,576]{0,1:T(8,128)(2,1)S(1)}, bf16[384,576]{0,1:T(8,128)(2,1)}, u32[]{:S(2)}, u32[]{:S(2)}) collective-permute-start(bf16[384,576]{0,1:T(8,128)(2,1)S(1)} %copy-done.6), channel_id=1, source_target_pairs={{0,16},{16,0},{32,48},{48,32},{64,80},{80,64},{96,112},{112,96},{1... | collective-permute-start | bytes 1327112 | tf_op jit(solution)/shard_map/ppermute | solution.py:70
  45.4 48.9 %collective-permute-start.1 = (bf16[384,576]{0,1:T(8,128)(2,1)S(1)}, bf16[384,576]{0,1:T(8,128)(2,1)}, u32[]{:S(2)}, u32[]{:S(2)}) collective-permute-start(bf16[384,576]{0,1:T(8,128)(2,1)S(1)} %copy-done.5), channel_id=1, source_target_pairs={{0,16},{16,0},{32,48},{48,32},{64,80},{80,64},{96,112},{112,96},{1... | collective-permute-start | bytes 1327112 | tf_op jit(solution)/shard_map/ppermute | solution.py:71
  97.2 6.9 %copy-start.7 = (bf16[576,384]{1,0:T(8,128)(2,1)S(1)}, bf16[576,384]{1,0:T(8,128)(2,1)}, u32[]{:S(2)}) copy-start(bf16[576,384]{1,0:T(8,128)(2,1)} %param.25) | copy-start | bytes 1327108
  97.2 23.5 %all-to-all-start.1 = ((bf16[16,16,2304]{2,1,0:T(8,128)(2,1)}), bf16[16,16,2304]{2,1,0:T(8,128)(2,1)S(1)}, u32[]{:S(2)}, u32[]{:S(2)}) async-start(bf16[16,16,2304]{2,1,0:T(8,128)(2,1)} %bitcast.9), calls=%async_computation.1 | async-start | bytes 2359296 | tf_op jit(solution)/shard_map/all_to_all | solution.py:109
  104.1 23.0 %collective-permute-start.2 = (bf16[576,384]{1,0:T(8,128)(2,1)S(1)}, bf16[576,384]{1,0:T(8,128)(2,1)S(1)}, u32[]{:S(2)}, u32[]{:S(2)}) collective-permute-start(bf16[576,384]{1,0:T(8,128)(2,1)S(1)} %copy-done.7), channel_id=1, source_target_pairs={{0,16},{16,0},{32,48},{48,32},{64,80},{80,64},{96,112},{112,96},{1... | collective-permute-start | bytes 1327112 | tf_op jit(solution)/shard_map/ppermute | solution.py:72
  121.8 15.3 %all-to-all-start.2 = ((bf16[16,16,1152]{2,1,0:T(8,128)(2,1)}), bf16[16,16,1152]{2,1,0:T(8,128)(2,1)S(1)}, u32[]{:S(2)}, u32[]{:S(2)}) async-start(bf16[16,16,1152]{2,1,0:T(8,128)(2,1)} %broadcast_in_dim.35), calls=%async_computation.2 | async-start | bytes 1179648 | tf_op jit(solution)/shard_map/all_to_all | solution.py:118
  137.6 10.9 %copy-start.1 = (bf16[256,512]{1,0:T(8,128)(2,1)S(1)}, bf16[256,512]{1,0:T(8,128)(2,1)}, u32[]{:S(2)}) copy-start(bf16[256,512]{1,0:T(8,128)(2,1)} %param.16) | copy-start | bytes 786436
  139.4 9.6 %copy-start.4 = (f32[256,2]{0,1:T(2,128)S(1)}, f32[256,2]{0,1:T(2,128)}, u32[]{:S(2)}) copy-start(f32[256,2]{0,1:T(2,128)} %param.21) | copy-start | bytes 6148
  139.4 55.8 %all-to-all-start.3 = ((bf16[64,2,1280]{2,1,0:T(2,128)(2,1)}), bf16[64,2,1280]{2,1,0:T(2,128)(2,1)S(1)}, u32[]{:S(2)}, u32[]{:S(2)}) async-start(bf16[64,2,1280]{2,1,0:T(2,128)(2,1)} %reshape.207), calls=%async_computation.3 | async-start | bytes 655360 | tf_op jit(solution)/shard_map/all_to_all | solution.py:130
  195.5 1.0 copy-start.9
  196.5 0.7 copy-start.3

commit v3 on v0

v3 whole, which is shorter than its diff:
```python
import jax
import jax.numpy as jnp
from jax import lax
from jax.experimental import pallas as pl
from jax.experimental.pallas import tpu as pltpu
from jax.sharding import PartitionSpec as P

EXP_FLY = 4
HIGHEST = lax.Precision.HIGHEST
INTERPRET = False


norm_eps = 1e-06


def dot(a, b, dims, precision=None):
    return lax.dot_general(
        a, b, (dims, ((), ())), precision=precision, preferred_element_type=jnp.float32
    )


NN = ((1,), (0,))
NT = ((1,), (1,))
TN = ((0,), (0,))


def iota(shape, axis):
    return lax.broadcasted_iota(jnp.int32, shape, axis)


def two_parts(x):
    high = x.astype(jnp.bfloat16)
    return high, (x - high.astype(jnp.float32)).astype(jnp.bfloat16)


def picks(place_ref, ids, block_rows, tokens):
    q = iota((block_rows, tokens), 0)
    per_expert = block_rows // EXP_FLY
    wanted = jnp.zeros((block_rows, tokens), jnp.int32)
    for j in range(EXP_FLY):
        here = (q >= j * per_expert) & (q < (j + 1) * per_expert)
        wanted = jnp.where(here, place_ref[j], wanted)
    first = ids[0:1, :] == wanted
    second = ids[1:2, :] == wanted
    match = jnp.where(first | second, 1.0, 0.0).astype(jnp.bfloat16)
    upto = jnp.where(iota((tokens, tokens), 0) <= iota((tokens, tokens), 1), 1.0, 0.0)
    count = dot(match, upto.astype(jnp.bfloat16), NN)
    slot = (2 * (q & 3)).astype(jnp.float32)
    found = match.astype(jnp.float32) > 0.5
    return found & (count == slot + 1.0), found & (count == slot + 2.0), first


def pre_kernel(place_ref, key_ref, value_ref, decay_ref, feat_ref, ids_ref, out_ref):
    tokens, feat = feat_ref.shape
    heads = decay_ref.shape[0]
    width = key_ref.shape[1] // heads
    block_rows = out_ref.shape[0]
    per_head = block_rows // heads
    chunks = width // per_head
    decay = decay_ref[...]
    after = jnp.where(iota((tokens, tokens), 1) > iota((tokens, tokens), 0), 1.0, 0.0)
    rest = dot(after, decay, NT, HIGHEST)
    pick_a, pick_b, _ = picks(place_ref, ids_ref[...], block_rows, tokens)
    features = feat_ref[...]
    for at, pick in ((0, pick_a), (feat, pick_b)):
        one_hot = jnp.where(pick, 1.0, 0.0).astype(jnp.bfloat16)
        out_ref[:, at : at + feat] = dot(one_hot, features, NN).astype(jnp.bfloat16)
    start = 2 * feat
    logs = jnp.zeros((block_rows, 64), jnp.float32)
    q = iota((block_rows, 64), 0)
    for h in range(heads):
        cols = slice(h * width, (h + 1) * width)
        value = value_ref[:, cols]
        high, low = two_parts(key_ref[:, cols].astype(jnp.float32) * jnp.exp(rest[:, h : h + 1]))
        state = dot(high, value, TN) + dot(low, value, TN)
        rows = slice(h * per_head, (h + 1) * per_head)
        for i in range(chunks):
            out_ref[rows, start + i * width : start + (i + 1) * width] = state[
                i * per_head : (i + 1) * per_head
            ].astype(jnp.bfloat16)
        total = jnp.sum(decay[h : h + 1, :], axis=1, keepdims=True)
        here = (q >= h * per_head) & (q < (h + 1) * per_head)
        logs = jnp.where(here, total, logs)
    high = logs.astype(jnp.bfloat16).astype(jnp.float32)
    mid = (logs - high).astype(jnp.bfloat16).astype(jnp.float32)
    lane = iota((block_rows, 64), 1)
    parts = jnp.where(lane == 0, high, jnp.where(lane == 1, mid, logs - high - mid))
    stop = start + chunks * width
    out_ref[:, stop : stop + 64] = jnp.where(lane < 3, parts, 0.0).astype(jnp.bfloat16)


def scan_kernel(piece_ref, log_ref, out_ref):
    n = out_ref.shape[0]
    logs = jnp.sum(log_ref[:, 0:3].astype(jnp.float32), axis=1, keepdims=True)
    row, col = iota((n, n), 0), iota((n, n), 1)
    row_block, col_block = row >> 1, col >> 1
    before = jnp.where((col_block < row_block) & ((col & 1) == 0), 1.0, 0.0)
    later = jnp.where(row_block > col_block, logs, 0.0)
    spans = dot(before, later, NN, HIGHEST)
    used = (col_block < row_block) & ((col & 1) == (row & 1))
    high, low = two_parts(jnp.where(used, jnp.exp(spans), 0.0))
    pieces = piece_ref[...]
    out_ref[...] = (dot(high, pieces, NN) + dot(low, pieces, NN)).astype(jnp.bfloat16)


def down_kernel(hidden_ref, own_ref, other_ref, state_ref, out_ref):
    half = out_ref.shape[0]
    ff, feat = own_ref.shape
    piece = dot(hidden_ref[:, :ff], own_ref[...], NN) + dot(hidden_ref[:, ff:], other_ref[...], NN)
    out_ref[:, :feat] = piece[:half].astype(jnp.bfloat16)
    out_ref[:, feat : 2 * feat] = piece[half:].astype(jnp.bfloat16)
    out_ref[:, 2 * feat :] = state_ref[...]


def side_kernel(
    place_ref,
    query_ref,
    key_ref,
    value_ref,
    gate_ref,
    decay_ref,
    gain_ref,
    ids_ref,
    route_ref,
    intra_ref,
    factor_ref,
    high_ref,
    low_ref,
    share_high_ref,
    share_low_ref,
):
    tokens = query_ref.shape[0]
    heads = decay_ref.shape[0]
    width = query_ref.shape[1] // heads
    block_rows = share_high_ref.shape[0] // 2
    decay = decay_ref[...]
    row, col = iota((tokens, tokens), 0), iota((tokens, tokens), 1)
    lower = row >= col
    cum_col = dot(jnp.where(lower, 1.0, 0.0), decay, NT, HIGHEST)
    cum_row = dot(decay, jnp.where(row <= col, 1.0, 0.0), NN, HIGHEST)
    for h in range(heads):
        cols = slice(h * width, (h + 1) * width)
        query = query_ref[:, cols]
        scores = dot(query, key_ref[:, cols], NT)
        spread = cum_col[:, h : h + 1] - cum_row[h : h + 1, :]
        weights = jnp.where(lower, jnp.exp(jnp.where(lower, spread, 0.0)), 0.0)
        intra_ref[:, cols] = dot((scores * weights).astype(jnp.bfloat16), value_ref[:, cols], NN)
        scaled = query.astype(jnp.float32) * jnp.exp(cum_col[:, h : h + 1])
        high_ref[:, cols], low_ref[:, cols] = two_parts(scaled)
    factor_ref[...] = gain_ref[...] / (1.0 + jnp.exp(-gate_ref[...].astype(jnp.float32)))
    pick_a, pick_b, first = picks(place_ref, ids_ref[...], block_rows, tokens)
    route = route_ref[...]
    weight = jnp.where(first, route[0:1, :], route[1:2, :])
    for at, pick in ((0, pick_a), (block_rows, pick_b)):
        rows = slice(at, at + block_rows)
        share_high_ref[rows, :], share_low_ref[rows, :] = two_parts(jnp.where(pick, weight, 0.0))


def post_kernel(
    back_ref,
    intra_ref,
    factor_ref,
    high_ref,
    low_ref,
    share_high_ref,
    share_low_ref,
    attention_ref,
    moe_ref,
):
    block_rows = back_ref.shape[0]
    feat = moe_ref.shape[1]
    total = None
    for at in range(2):
        rows = slice(at * block_rows, (at + 1) * block_rows)
        pieces = back_ref[:, at * feat : (at + 1) * feat]
        part = dot(share_high_ref[rows, :], pieces, TN) + dot(share_low_ref[rows, :], pieces, TN)
        total = part if total is None else total + part
    moe_ref[...] = total.astype(jnp.bfloat16)
    width = 128
    heads = attention_ref.shape[1] // width
    per_head = block_rows // heads
    chunks = width // per_head
    for h in range(heads):
        cols = slice(h * width, (h + 1) * width)
        rows = slice(h * per_head, (h + 1) * per_head)
        state = jnp.concatenate(
            [
                back_ref[rows, 2 * feat + i * width : 2 * feat + (i + 1) * width]
                for i in range(chunks)
            ],
            axis=0,
        )
        mixed = (
            intra_ref[:, cols]
            + dot(high_ref[:, cols], state, NN)
            + dot(low_ref[:, cols], state, NN)
        )
        power = jnp.sum(mixed * mixed, axis=1, keepdims=True) * (1.0 / width)
        attention_ref[:, cols] = (mixed * lax.rsqrt(power + norm_eps) * factor_ref[:, cols]).astype(
            jnp.bfloat16
        )


def call(kernel, outs, scalars, cost, *arrays):
    specs = [pl.BlockSpec(memory_space=pltpu.SMEM)] * scalars
    specs += [pl.BlockSpec(memory_space=pltpu.VMEM)] * (len(arrays) - scalars)
    out_specs = [pl.BlockSpec(memory_space=pltpu.VMEM)] * len(outs)
    out_shape = [jax.ShapeDtypeStruct(shape, kind) for shape, kind in outs]
    if len(outs) == 1:
        out_specs, out_shape = out_specs[0], out_shape[0]
    return pl.pallas_call(
        kernel,
        in_specs=specs,
        out_specs=out_specs,
        out_shape=out_shape,
        cost_estimate=pl.CostEstimate(flops=cost, bytes_accessed=cost // 256, transcendentals=0),
        interpret=INTERPRET,
    )(*arrays)


def per_device(
    queries,
    key_input,
    value_input,
    out_gate,
    log_decay,
    norm_gain,
    features,
    expert_ids,
    route_weight,
    placement,
    gate_weight,
    up_weight,
    down_weight,
):
    seq_count = lax.axis_size("seq")
    head_count = lax.axis_size("head")
    tokens = queries.shape[0]
    heads_here = log_decay.shape[0]
    width = queries.shape[1] // heads_here
    feat = features.shape[1]
    ff = gate_weight.shape[1]
    bf16, f32 = jnp.bfloat16, jnp.float32
    lines = 2 * seq_count
    state_len = heads_here * width * width // lines
    ids = expert_ids.T
    swap = [(i, i ^ 1) for i in range(seq_count)]

    outgoing = call(
        pre_kernel,
        [((lines, 2 * feat + state_len + 64), bf16)],
        1,
        2**28,
        placement,
        key_input,
        value_input,
        log_decay,
        features,
        ids,
    )
    other_gate = lax.ppermute(gate_weight, "seq", swap)
    other_up = lax.ppermute(up_weight, "seq", swap)
    other_down = lax.ppermute(down_weight, "seq", swap)
    arrived = lax.all_to_all(
        outgoing.reshape(seq_count, 2, -1), "seq", split_axis=0, concat_axis=0, tiled=True
    ).reshape(lines, -1)

    slot_rows = jnp.concatenate([arrived[:, :feat], arrived[:, feat : 2 * feat]], axis=0)
    both_weight = jnp.concatenate([gate_weight, other_gate, up_weight, other_up], axis=1)
    gate_up = jnp.dot(slot_rows, both_weight, preferred_element_type=f32).astype(bf16)
    rows = slot_rows.shape[0]
    parts = lax.all_to_all(
        gate_up.reshape(head_count, rows // head_count, 4 * ff),
        "head",
        split_axis=0,
        concat_axis=0,
        tiled=True,
    )
    prefix_piece = call(
        scan_kernel,
        [((lines, state_len), bf16)],
        0,
        2**26,
        arrived[:, 2 * feat : 2 * feat + state_len],
        arrived[:, 2 * feat + state_len :],
    )
    summed = jnp.sum(parts.astype(f32), axis=0)
    hidden_part = (jax.nn.silu(summed[:, : 2 * ff]) * summed[:, 2 * ff :]).astype(bf16)
    hidden = lax.all_to_all(
        jnp.broadcast_to(hidden_part[None], (head_count,) + hidden_part.shape),
        "head",
        split_axis=0,
        concat_axis=0,
        tiled=True,
    ).reshape(rows, 2 * ff)
    leaving = call(
        down_kernel,
        [((lines, 2 * feat + state_len), bf16)],
        0,
        2**28,
        hidden,
        down_weight,
        other_down,
        prefix_piece,
    )
    returned = lax.all_to_all(
        leaving.reshape(seq_count, 2, -1), "seq", split_axis=0, concat_axis=0, tiled=True
    ).reshape(lines, -1)
    side = call(
        side_kernel,
        [
            ((tokens, heads_here * width), f32),
            ((tokens, heads_here * width), f32),
            ((tokens, heads_here * width), bf16),
            ((tokens, heads_here * width), bf16),
            ((2 * lines, tokens), bf16),
            ((2 * lines, tokens), bf16),
        ],
        1,
        2**29,
        placement,
        queries,
        key_input,
        value_input,
        out_gate,
        log_decay,
        norm_gain.reshape(1, -1),
        ids,
        route_weight.T,
    )
    attention_out, moe_out = call(
        post_kernel,
        [((tokens, heads_here * width), bf16), ((tokens, feat), bf16)],
        0,
        2**28,
        returned,
        *side,
    )
    return (attention_out, moe_out)


def solution(mesh):
    placed = (
        P("seq", "head"),
        P("seq", "head"),
        P("seq", "head"),
        P("seq", "head"),
        P("head", "seq"),
        P("head"),
        P("seq", "head"),
        P("seq", None),
        P("seq", None),
        P(),
        P("head", "seq"),
        P("head", "seq"),
        P("seq", "head"),
    )

    return jax.shard_map(
        per_device,
        mesh=mesh,
        in_specs=placed,
        out_specs=(P("seq", "head"), P("seq", "head")),
        check_vma=False,
    )
```

time: 540 us -> 191 us (0.35)
  the two profiles are of different devices: /device:TPU:993 before, /device:TPU:1 now
where the time goes in v3:
time: 191 us; the launch traced here: 190 us
  waiting for transfers between devices  91.3 us (48%)
  starting transfers between devices  51.3 us (27%)
  blocking collectives  23.5 us (12%)
  Pallas kernels  14.3 us (7%)
  local copies, waits for them, and re-layouts  7.8 us (4%)
    all_to_all x1, waiting for transfers between devices, per_device(): lax.all_to_all(outgoing.reshape(seq_count, 2, -1), 'seq', split_axis=0, c...  46.2 us
    all_to_all x1, waiting for transfers between devices, per_device(): lax.all_to_all(leaving.reshape(seq_count, 2, -1), 'seq', split_axis=0, co...  43.2 us
    all_to_all x1, starting transfers between devices, per_device(): lax.all_to_all(outgoing.reshape(seq_count, 2, -1), 'seq', split_axis=0, c...  30.4 us
    all_to_all x1, blocking collectives, per_device(): lax.all_to_all(gate_up.reshape(head_count, rows // head_count, 4 * ff), '...  23.5 us
    pallas_call x5, Pallas kernels, call(): pl.pallas_call(kernel, in_specs=specs, out_specs=out_specs, out_shape=out...  14.3 us
    all_to_all x1, starting transfers between devices, per_device(): lax.all_to_all(leaving.reshape(seq_count, 2, -1), 'seq', split_axis=0, co...  8.47 us
    ppermute x1, starting transfers between devices, per_device(): other_down = lax.ppermute(down_weight, 'seq', swap)  4.54 us
  transfers between devices with their start and end apart: 6, of which 3 were waited for; matrix products, arithmetic and copies ran while one was open for 1% of the time, Pallas kernels for 3%

profile of v3, /device:TPU:1, one launch (start us, length us, event | category | flops | bytes accessed | tf_op | source)
XLA Modules:
  0.0 190.0 jit_solution(6249621637379780469)
XLA Ops:
  0.7 3.1 %shard_map.140 = bf16[128,1344]{1,0:T(8,128)(2,1)} custom-call(s32[4]{0:T(128)} %place_ref.3, bf16[256,512]{1,0:T(8,128)(2,1)} %key_ref.3, bf16[256,512]{1,0:T(8,128)(2,1)} %value_ref.3, f32[4,256]{1,0:T(4,128)} %decay_ref.3, bf16[256,384]{1,0:T(8,128)(2,1)} %feat_ref.1, s32[2,256]{1,0:T(2,128)} %bitcast.7), custom_call_target="tpu_custom_call" | custom-call | flops 268435456 | bytes 1048576 | tf_op jit(solution)/shard_map/pallas_call | solution.py:211
  3.8 1.9 reshape.26
  5.6 30.4 %all-to-all-start = ((bf16[64,2,1344]{2,1,0:T(2,128)(2,1)}), bf16[64,2,1344]{2,1,0:T(2,128)(2,1)S(1)}, u32[]{:S(2)}, u32[]{:S(2)}) async-start(bf16[64,2,1344]{2,1,0:T(2,128)(2,1)} %reshape.26), calls=%async_computation | async-start | bytes 720896 | tf_op jit(solution)/shard_map/all_to_all | solution.py:264
  36.0 2.4 %collective-permute-start = (bf16[384,576]{0,1:T(8,128)(2,1)S(1)}, bf16[384,576]{0,1:T(8,128)(2,1)S(1)}, u32[]{:S(2)}, u32[]{:S(2)}) collective-permute-start(bf16[384,576]{0,1:T(8,128)(2,1)S(1)} %copy-done.4), channel_id=1, source_target_pairs={{0,16},{16,0},{32,48},{48,32},{64,80},{80,64},{96,112},{112,96},{1... | collective-permute-start | bytes 1327112 | tf_op jit(solution)/shard_map/ppermute | solution.py:261
  38.4 2.0 %collective-permute-start.1 = (bf16[384,576]{0,1:T(8,128)(2,1)S(1)}, bf16[384,576]{0,1:T(8,128)(2,1)S(1)}, u32[]{:S(2)}, u32[]{:S(2)}) collective-permute-start(bf16[384,576]{0,1:T(8,128)(2,1)S(1)} %copy-done.3), channel_id=1, source_target_pairs={{0,16},{16,0},{32,48},{48,32},{64,80},{80,64},{96,112},{112,96},{1... | collective-permute-start | bytes 1327112 | tf_op jit(solution)/shard_map/ppermute | solution.py:262
  40.4 46.2 %all-to-all-done = bf16[64,2,1344]{2,1,0:T(2,128)(2,1)S(1)} async-done(((bf16[64,2,1344]{2,1,0:T(2,128)(2,1)}), bf16[64,2,1344]{2,1,0:T(2,128)(2,1)S(1)}, u32[]{:S(2)}, u32[]{:S(2)}) %all-to-all-start) | async-done | bytes 344096 | tf_op jit(solution)/shard_map/all_to_all | solution.py:264
  86.6 0.3 reshape.27
  86.9 0.8 convolution_convert_fusion
  87.7 23.5 %all_to_all.20 = bf16[16,16,2304]{2,1,0:T(8,128)(2,1)S(1)} all-to-all(bf16[16,16,2304]{2,1,0:T(8,128)(2,1)S(1)} %bitcast.6), channel_id=1, replica_groups=mesh['seq'=64,'head'=16] {'head'}, dimensions={0} | all-to-all | bytes 2359296 | tf_op jit(solution)/shard_map/all_to_all | solution.py:272
  111.5 0.9 broadcast_in_dim.2
  112.3 3.6 %all-to-all-start.2 = ((bf16[16,16,1152]{2,1,0:T(8,128)(2,1)}), bf16[16,16,1152]{2,1,0:T(8,128)(2,1)S(1)}, u32[]{:S(2)}, u32[]{:S(2)}) async-start(bf16[16,16,1152]{2,1,0:T(8,128)(2,1)} %broadcast_in_dim.2), calls=%async_computation.2 | async-start | bytes 1179648 | tf_op jit(solution)/shard_map/all_to_all | solution.py:289
  115.9 4.5 %collective-permute-start.2 = (bf16[576,384]{1,0:T(8,128)(2,1)S(1)}, bf16[576,384]{1,0:T(8,128)(2,1)S(1)}, u32[]{:S(2)}, u32[]{:S(2)}) collective-permute-start(bf16[576,384]{1,0:T(8,128)(2,1)S(1)} %copy-done.1), channel_id=1, source_target_pairs={{0,16},{16,0},{32,48},{48,32},{64,80},{80,64},{96,112},{112,96},{1... | collective-permute-start | bytes 1327112 | tf_op jit(solution)/shard_map/ppermute | solution.py:263
  120.5 0.6 slice.29.log_ref
  121.1 0.7 slice.28.piece_ref
  121.8 2.1 %shard_map.141.state_ref = bf16[128,512]{1,0:T(8,128)(2,1)} custom-call(bf16[128,512]{1,0:T(8,128)(2,1)} %slice.28.piece_ref, bf16[128,64]{1,0:T(8,128)(2,1)} %slice.29.log_ref), custom_call_target="tpu_custom_call" | custom-call | flops 67108864 | bytes 262144 | tf_op jit(solution)/shard_map/pallas_call | solution.py:211
  123.9 1.9 all-to-all-done.2
  125.7 0.8 copy-done
  126.6 2.7 %shard_map.142 = bf16[128,1280]{1,0:T(8,128)(2,1)} custom-call(bf16[256,1152]{1,0:T(8,128)(2,1)} %bitcast.5, bf16[576,384]{1,0:T(8,128)(2,1)} %own_ref.1, bf16[576,384]{1,0:T(8,128)(2,1)} %copy-done.2, bf16[128,512]{1,0:T(8,128)(2,1)} %shard_map.141.state_ref), custom_call_target="tpu_custom_call" | custom-call | flops 268435456 | bytes 1048576 | tf_op jit(solution)/shard_map/pallas_call | solution.py:211
  129.2 1.8 reshape.30
  131.0 8.5 %all-to-all-start.3 = ((bf16[64,2,1280]{2,1,0:T(2,128)(2,1)}), bf16[64,2,1280]{2,1,0:T(2,128)(2,1)S(1)}, u32[]{:S(2)}, u32[]{:S(2)}) async-start(bf16[64,2,1280]{2,1,0:T(2,128)(2,1)} %reshape.30), calls=%async_computation.3 | async-start | bytes 655360 | tf_op jit(solution)/shard_map/all_to_all | solution.py:306
  139.5 3.5 %shard_map.143 = (f32[256,512]{1,0:T(8,128)}, f32[256,512]{1,0:T(8,128)}, bf16[256,512]{1,0:T(8,128)(2,1)}, bf16[256,512]{1,0:T(8,128)(2,1)}, bf16[256,256]{1,0:T(8,128)(2,1)}, /*index=5*/bf16[256,256]{1,0:T(8,128)(2,1)}) custom-call(s32[4]{0:T(128)} %place_ref.3, bf16[256,512]{1,0:T(8,128)(2,1)} %query_ref.1, bf16[256,512]{1,0:T(8,128)(2,1)} %key_ref.3, ...), custom_call_target="tpu_custom_call" | custom-call | flops 536870912 | bytes 2097152 | tf_op jit(solution)/shard_map/pallas_call | solution.py:211
  143.0 43.2 %all-to-all-done.3 = bf16[64,2,1280]{2,1,0:T(2,128)(2,1)S(1)} async-done(((bf16[64,2,1280]{2,1,0:T(2,128)(2,1)}), bf16[64,2,1280]{2,1,0:T(2,128)(2,1)S(1)}, u32[]{:S(2)}, u32[]{:S(2)}) %all-to-all-start.3) | async-done | bytes 327712 | tf_op jit(solution)/shard_map/all_to_all | solution.py:306
  186.2 0.9 reshape.31.back_ref
  187.1 2.9 %shard_map.144 = (bf16[256,512]{1,0:T(8,128)(2,1)}, bf16[256,384]{1,0:T(8,128)(2,1)}) custom-call(bf16[128,1280]{1,0:T(8,128)(2,1)} %reshape.31.back_ref, f32[256,512]{1,0:T(8,128)} %get-tuple-element.8.intra_ref, f32[256,512]{1,0:T(8,128)} %get-tuple-element.9.factor_ref, bf16[256,512]{1,0:T(8,128)(2,1)} %get-tuple-element.10.high_ref, ...), custom_call_target="tpu_custom_call" | custom-call | flops 268435456 | bytes 1048576 | tf_op jit(solution)/shard_map/pallas_call | solution.py:211
  (15 shorter events, 0.2 us)
Async XLA Ops:
  0.6 35.4 %copy-start.4 = (bf16[384,576]{0,1:T(8,128)(2,1)S(1)}, bf16[384,576]{0,1:T(8,128)(2,1)}, u32[]{:S(2)}) copy-start(bf16[384,576]{0,1:T(8,128)(2,1)} %param.23) | copy-start | bytes 1327108
  0.6 37.8 %copy-start.3 = (bf16[384,576]{0,1:T(8,128)(2,1)S(1)}, bf16[384,576]{0,1:T(8,128)(2,1)}, u32[]{:S(2)}) copy-start(bf16[384,576]{0,1:T(8,128)(2,1)} %param.24) | copy-start | bytes 1327108
  5.6 81.0 %all-to-all-start = ((bf16[64,2,1344]{2,1,0:T(2,128)(2,1)}), bf16[64,2,1344]{2,1,0:T(2,128)(2,1)S(1)}, u32[]{:S(2)}, u32[]{:S(2)}) async-start(bf16[64,2,1344]{2,1,0:T(2,128)(2,1)} %reshape.26), calls=%async_computation | async-start | bytes 720896 | tf_op jit(solution)/shard_map/all_to_all | solution.py:264
  36.0 50.9 %collective-permute-start = (bf16[384,576]{0,1:T(8,128)(2,1)S(1)}, bf16[384,576]{0,1:T(8,128)(2,1)S(1)}, u32[]{:S(2)}, u32[]{:S(2)}) collective-permute-start(bf16[384,576]{0,1:T(8,128)(2,1)S(1)} %copy-done.4), channel_id=1, source_target_pairs={{0,16},{16,0},{32,48},{48,32},{64,80},{80,64},{96,112},{112,96},{1... | collective-permute-start | bytes 1327112 | tf_op jit(solution)/shard_map/ppermute | solution.py:261
  38.4 48.5 %collective-permute-start.1 = (bf16[384,576]{0,1:T(8,128)(2,1)S(1)}, bf16[384,576]{0,1:T(8,128)(2,1)S(1)}, u32[]{:S(2)}, u32[]{:S(2)}) collective-permute-start(bf16[384,576]{0,1:T(8,128)(2,1)S(1)} %copy-done.3), channel_id=1, source_target_pairs={{0,16},{16,0},{32,48},{48,32},{64,80},{80,64},{96,112},{112,96},{1... | collective-permute-start | bytes 1327112 | tf_op jit(solution)/shard_map/ppermute | solution.py:262
  111.4 4.5 %copy-start.1 = (bf16[576,384]{1,0:T(8,128)(2,1)S(1)}, bf16[576,384]{1,0:T(8,128)(2,1)}, u32[]{:S(2)}) copy-start(bf16[576,384]{1,0:T(8,128)(2,1)} %own_ref.1) | copy-start | bytes 1327108
  112.3 13.4 %all-to-all-start.2 = ((bf16[16,16,1152]{2,1,0:T(8,128)(2,1)}), bf16[16,16,1152]{2,1,0:T(8,128)(2,1)S(1)}, u32[]{:S(2)}, u32[]{:S(2)}) async-start(bf16[16,16,1152]{2,1,0:T(8,128)(2,1)} %broadcast_in_dim.2), calls=%async_computation.2 | async-start | bytes 1179648 | tf_op jit(solution)/shard_map/all_to_all | solution.py:289
  115.9 7.9 %collective-permute-start.2 = (bf16[576,384]{1,0:T(8,128)(2,1)S(1)}, bf16[576,384]{1,0:T(8,128)(2,1)S(1)}, u32[]{:S(2)}, u32[]{:S(2)}) collective-permute-start(bf16[576,384]{1,0:T(8,128)(2,1)S(1)} %copy-done.1), channel_id=1, source_target_pairs={{0,16},{16,0},{32,48},{48,32},{64,80},{80,64},{96,112},{112,96},{1... | collective-permute-start | bytes 1327112 | tf_op jit(solution)/shard_map/ppermute | solution.py:263
  123.9 1.9 copy-start.2
  125.7 0.8 copy-start
  131.0 55.2 %all-to-all-start.3 = ((bf16[64,2,1280]{2,1,0:T(2,128)(2,1)}), bf16[64,2,1280]{2,1,0:T(2,128)(2,1)S(1)}, u32[]{:S(2)}, u32[]{:S(2)}) async-start(bf16[64,2,1280]{2,1,0:T(2,128)(2,1)} %reshape.30), calls=%async_computation.3 | async-start | bytes 655360 | tf_op jit(solution)/shard_map/all_to_all | solution.py:306

commit v4 on v3

--- a/solution.py
+++ b/solution.py
@@ -45,27 +45,28 @@
     match = jnp.where(first | second, 1.0, 0.0).astype(jnp.bfloat16)
     upto = jnp.where(iota((tokens, tokens), 0) <= iota((tokens, tokens), 1), 1.0, 0.0)
     count = dot(match, upto.astype(jnp.bfloat16), NN)
-    slot = (2 * (q & 3)).astype(jnp.float32)
-    found = match.astype(jnp.float32) > 0.5
-    return found & (count == slot + 1.0), found & (count == slot + 2.0), first
+    slot = (2 * (q & 2) + ((q & 4) >> 1) + (q & 1)).astype(jnp.float32)
+    return (match.astype(jnp.float32) > 0.5) & (count == slot + 1.0), first
+
+
+def in_pairs(x):
+    return x.reshape(x.shape[0] // 2, 2, x.shape[1]).astype(jnp.bfloat16)
 
 
 def pre_kernel(place_ref, key_ref, value_ref, decay_ref, feat_ref, ids_ref, out_ref):
     tokens, feat = feat_ref.shape
     heads = decay_ref.shape[0]
     width = key_ref.shape[1] // heads
-    block_rows = out_ref.shape[0]
+    block_rows = 2 * out_ref.shape[0]
     per_head = block_rows // heads
     chunks = width // per_head
     decay = decay_ref[...]
     after = jnp.where(iota((tokens, tokens), 1) > iota((tokens, tokens), 0), 1.0, 0.0)
     rest = dot(after, decay, NT, HIGHEST)
-    pick_a, pick_b, _ = picks(place_ref, ids_ref[...], block_rows, tokens)
-    features = feat_ref[...]
-    for at, pick in ((0, pick_a), (feat, pick_b)):
-        one_hot = jnp.where(pick, 1.0, 0.0).astype(jnp.bfloat16)
-        out_ref[:, at : at + feat] = dot(one_hot, features, NN).astype(jnp.bfloat16)
-    start = 2 * feat
+    pick, _ = picks(place_ref, ids_ref[...], block_rows, tokens)
+    one_hot = jnp.where(pick, 1.0, 0.0).astype(jnp.bfloat16)
+    out_ref[:, :, :feat] = in_pairs(dot(one_hot, feat_ref[...], NN))
+    start = feat
     logs = jnp.zeros((block_rows, 64), jnp.float32)
     q = iota((block_rows, 64), 0)
     for h in range(heads):
@@ -73,11 +74,11 @@
         value = value_ref[:, cols]
         high, low = two_parts(key_ref[:, cols].astype(jnp.float32) * jnp.exp(rest[:, h : h + 1]))
         state = dot(high, value, TN) + dot(low, value, TN)
-        rows = slice(h * per_head, (h + 1) * per_head)
+        rows = slice(h * per_head // 2, (h + 1) * per_head // 2)
         for i in range(chunks):
-            out_ref[rows, start + i * width : start + (i + 1) * width] = state[
-                i * per_head : (i + 1) * per_head
-            ].astype(jnp.bfloat16)
+            out_ref[rows, :, start + i * width : start + (i + 1) * width] = in_pairs(
+                state[i * per_head : (i + 1) * per_head]
+            )
         total = jnp.sum(decay[h : h + 1, :], axis=1, keepdims=True)
         here = (q >= h * per_head) & (q < (h + 1) * per_head)
         logs = jnp.where(here, total, logs)
@@ -86,7 +87,7 @@
     lane = iota((block_rows, 64), 1)
     parts = jnp.where(lane == 0, high, jnp.where(lane == 1, mid, logs - high - mid))
     stop = start + chunks * width
-    out_ref[:, stop : stop + 64] = jnp.where(lane < 3, parts, 0.0).astype(jnp.bfloat16)
+    out_ref[:, :, stop : stop + 64] = in_pairs(jnp.where(lane < 3, parts, 0.0))
 
 
 def scan_kernel(piece_ref, log_ref, out_ref):
@@ -101,15 +102,6 @@
     high, low = two_parts(jnp.where(used, jnp.exp(spans), 0.0))
     pieces = piece_ref[...]
     out_ref[...] = (dot(high, pieces, NN) + dot(low, pieces, NN)).astype(jnp.bfloat16)
-
-
-def down_kernel(hidden_ref, own_ref, other_ref, state_ref, out_ref):
-    half = out_ref.shape[0]
-    ff, feat = own_ref.shape
-    piece = dot(hidden_ref[:, :ff], own_ref[...], NN) + dot(hidden_ref[:, ff:], other_ref[...], NN)
-    out_ref[:, :feat] = piece[:half].astype(jnp.bfloat16)
-    out_ref[:, feat : 2 * feat] = piece[half:].astype(jnp.bfloat16)
-    out_ref[:, 2 * feat :] = state_ref[...]
 
 
 def side_kernel(
@@ -132,7 +124,7 @@
     tokens = query_ref.shape[0]
     heads = decay_ref.shape[0]
     width = query_ref.shape[1] // heads
-    block_rows = share_high_ref.shape[0] // 2
+    block_rows = share_high_ref.shape[0]
     decay = decay_ref[...]
     row, col = iota((tokens, tokens), 0), iota((tokens, tokens), 1)
     lower = row >= col
@@ -148,12 +140,10 @@
         scaled = query.astype(jnp.float32) * jnp.exp(cum_col[:, h : h + 1])
         high_ref[:, cols], low_ref[:, cols] = two_parts(scaled)
     factor_ref[...] = gain_ref[...] / (1.0 + jnp.exp(-gate_ref[...].astype(jnp.float32)))
-    pick_a, pick_b, first = picks(place_ref, ids_ref[...], block_rows, tokens)
+    pick, first = picks(place_ref, ids_ref[...], block_rows, tokens)
     route = route_ref[...]
     weight = jnp.where(first, route[0:1, :], route[1:2, :])
-    for at, pick in ((0, pick_a), (block_rows, pick_b)):
-        rows = slice(at, at + block_rows)
-        share_high_ref[rows, :], share_low_ref[rows, :] = two_parts(jnp.where(pick, weight, 0.0))
+    share_high_ref[...], share_low_ref[...] = two_parts(jnp.where(pick, weight, 0.0))
 
 
 def post_kernel(
@@ -169,12 +159,8 @@
 ):
     block_rows = back_ref.shape[0]
     feat = moe_ref.shape[1]
-    total = None
-    for at in range(2):
-        rows = slice(at * block_rows, (at + 1) * block_rows)
-        pieces = back_ref[:, at * feat : (at + 1) * feat]
-        part = dot(share_high_ref[rows, :], pieces, TN) + dot(share_low_ref[rows, :], pieces, TN)
-        total = part if total is None else total + part
+    pieces = back_ref[:, :feat]
+    total = dot(share_high_ref[...], pieces, TN) + dot(share_low_ref[...], pieces, TN)
     moe_ref[...] = total.astype(jnp.bfloat16)
     width = 128
     heads = attention_ref.shape[1] // width
@@ -185,7 +171,7 @@
         rows = slice(h * per_head, (h + 1) * per_head)
         state = jnp.concatenate(
             [
-                back_ref[rows, 2 * feat + i * width : 2 * feat + (i + 1) * width]
+                back_ref[rows, feat + i * width : feat + (i + 1) * width]
                 for i in range(chunks)
             ],
             axis=0,
@@ -245,10 +231,11 @@
     state_len = heads_here * width * width // lines
     ids = expert_ids.T
     swap = [(i, i ^ 1) for i in range(seq_count)]
+    next_chip = [(i, i ^ 2) for i in range(seq_count)]
 
     outgoing = call(
         pre_kernel,
-        [((lines, 2 * feat + state_len + 64), bf16)],
+        [((seq_count, 2, feat + state_len + 64), bf16)],
         1,
         2**28,
         placement,
@@ -262,10 +249,12 @@
     other_up = lax.ppermute(up_weight, "seq", swap)
     other_down = lax.ppermute(down_weight, "seq", swap)
     arrived = lax.all_to_all(
-        outgoing.reshape(seq_count, 2, -1), "seq", split_axis=0, concat_axis=0, tiled=True
+        outgoing, "seq", split_axis=0, concat_axis=0, tiled=True
     ).reshape(lines, -1)
 
-    slot_rows = jnp.concatenate([arrived[:, :feat], arrived[:, feat : 2 * feat]], axis=0)
+    own_rows = arrived[:, :feat]
+    near_rows = lax.ppermute(own_rows, "seq", next_chip)
+    slot_rows = jnp.concatenate([own_rows, near_rows], axis=0)
     both_weight = jnp.concatenate([gate_weight, other_gate, up_weight, other_up], axis=1)
     gate_up = jnp.dot(slot_rows, both_weight, preferred_element_type=f32).astype(bf16)
     rows = slot_rows.shape[0]
@@ -281,8 +270,8 @@
         [((lines, state_len), bf16)],
         0,
         2**26,
-        arrived[:, 2 * feat : 2 * feat + state_len],
-        arrived[:, 2 * feat + state_len :],
+        arrived[:, feat : feat + state_len],
+        arrived[:, feat + state_len :],
     )
     summed = jnp.sum(parts.astype(f32), axis=0)
     hidden_part = (jax.nn.silu(summed[:, : 2 * ff]) * summed[:, 2 * ff :]).astype(bf16)
@@ -293,16 +282,14 @@
         concat_axis=0,
         tiled=True,
     ).reshape(rows, 2 * ff)
-    leaving = call(
-        down_kernel,
-        [((lines, 2 * feat + state_len), bf16)],
-        0,
-        2**28,
+    piece = jnp.dot(
         hidden,
-        down_weight,
-        other_down,
-        prefix_piece,
-    )
+        jnp.concatenate([down_weight, other_down], axis=0),
+        preferred_element_type=f32,
+    ).astype(bf16)
+    near_piece = lax.ppermute(piece[lines:], "seq", next_chip)
+    piece = (piece[:lines].astype(f32) + near_piece.astype(f32)).astype(bf16)
+    leaving = jnp.concatenate([piece, prefix_piece], axis=1)
     returned = lax.all_to_all(
         leaving.reshape(seq_count, 2, -1), "seq", split_axis=0, concat_axis=0, tiled=True
     ).reshape(lines, -1)
@@ -313,8 +300,8 @@
             ((tokens, heads_here * width), f32),
             ((tokens, heads_here * width), bf16),
             ((tokens, heads_here * width), bf16),
-            ((2 * lines, tokens), bf16),
-            ((2 * lines, tokens), bf16),
+            ((lines, tokens), bf16),
+            ((lines, tokens), bf16),
         ],
         1,
         2**29,

time: 191 us -> 181 us (0.948)
  waiting for transfers between devices: 91.3 us -> 77.1 us
  starting transfers between devices: 51.3 us -> 63.1 us
  local copies, waits for them, and re-layouts: 7.8 us -> 3.92 us
  Pallas kernels: 14.3 us -> 11.3 us
  blocking collectives: 23.5 us -> 21.4 us
    all_to_all x1, waiting for transfers between devices: 46.2 us -> 36.9 us  [per_device(): lax.all_to_all(outgoing, 'seq', split_axis=0, concat_axis=0, tiled=True)]
    all_to_all x1, waiting for transfers between devices: 43.2 us -> 35.4 us  [per_device(): lax.all_to_all(leaving.reshape(seq_count, 2, -1), 'seq', split_axis=0, co...]
    ppermute x0 -> x2, starting transfers between devices: none -> 7.53 us  [the longest x1 4.26 us: per_device(): near_piece = lax.ppermute(piece[lines:], 'seq', next_chip)]
    pallas_call x5 -> x4, Pallas kernels: 14.3 us -> 11.3 us  [call(): pl.pallas_call(kernel, in_specs=specs, out_specs=out_specs, out_shape=out...]
    all_to_all x1, starting transfers between devices: 8.47 us -> 10.6 us  [per_device(): lax.all_to_all(leaving.reshape(seq_count, 2, -1), 'seq', split_axis=0, co...]
    all_to_all x1, blocking collectives: 23.5 us -> 21.4 us  [per_device(): lax.all_to_all(gate_up.reshape(head_count, rows // head_count, 4 * ff), '...]
    ppermute x1, starting transfers between devices: 4.54 us -> 6.63 us  [per_device(): other_down = lax.ppermute(down_weight, 'seq', swap)]
    ppermute x0 -> x2, waiting for transfers between devices: none -> 2.06 us  [the longest x1 2.06 us: per_device(): near_rows = lax.ppermute(own_rows, 'seq', next_chip)]
  transfers between devices with their start and end apart: 6 -> 8, of which waited for: 3 -> 5; matrix products, arithmetic and copies ran while one was open for 1% -> 1% of each run, Pallas kernels for 3% -> 3%
where the time goes in v4:
time: 181 us; the launch traced here: 180 us
  waiting for transfers between devices  77.1 us (43%)
  starting transfers between devices  63.1 us (35%)
  blocking collectives  21.4 us (12%)
  Pallas kernels  11.3 us (6%)
  local copies, waits for them, and re-layouts  3.92 us (2%)
    all_to_all x1, waiting for transfers between devices, per_device(): lax.all_to_all(outgoing, 'seq', split_axis=0, concat_axis=0, tiled=True)  36.9 us
    all_to_all x1, waiting for transfers between devices, per_device(): lax.all_to_all(leaving.reshape(seq_count, 2, -1), 'seq', split_axis=0, co...  35.4 us
    all_to_all x1, starting transfers between devices, per_device(): lax.all_to_all(outgoing, 'seq', split_axis=0, concat_axis=0, tiled=True)  30.4 us
    all_to_all x1, blocking collectives, per_device(): lax.all_to_all(gate_up.reshape(head_count, rows // head_count, 4 * ff), '...  21.4 us
    pallas_call x4, Pallas kernels, call(): pl.pallas_call(kernel, in_specs=specs, out_specs=out_specs, out_shape=out...  11.3 us
    all_to_all x1, starting transfers between devices, per_device(): lax.all_to_all(leaving.reshape(seq_count, 2, -1), 'seq', split_axis=0, co...  10.6 us
    ppermute x1, starting transfers between devices, per_device(): other_down = lax.ppermute(down_weight, 'seq', swap)  6.63 us
    ppermute x1, starting transfers between devices, per_device(): near_piece = lax.ppermute(piece[lines:], 'seq', next_chip)  4.26 us
  transfers between devices with their start and end apart: 8, of which 5 were waited for; matrix products, arithmetic and copies ran while one was open for 1% of the time, Pallas kernels for 3%

profile of v4, /device:TPU:1, one launch (start us, length us, event | category | flops | bytes accessed | tf_op | source)
XLA Modules:
  0.0 180.0 jit_solution(3509854245443428876)
XLA Ops:
  0.7 3.0 %shard_map.140 = bf16[64,2,960]{2,1,0:T(2,128)(2,1)} custom-call(s32[4]{0:T(128)} %place_ref.3, bf16[256,512]{1,0:T(8,128)(2,1)} %key_ref.3, bf16[256,512]{1,0:T(8,128)(2,1)} %value_ref.3, f32[4,256]{1,0:T(4,128)} %decay_ref.3, bf16[256,384]{1,0:T(8,128)(2,1)} %feat_ref.1, s32[2,256]{1,0:T(2,128)} %bitcast.8), custom_call_target="tpu_custom_call" | custom-call | flops 268435456 | bytes 1048576 | tf_op jit(solution)/shard_map/pallas_call | solution.py:197
  3.7 30.4 %all-to-all-start = ((bf16[64,2,960]{2,1,0:T(2,128)(2,1)}), bf16[64,2,960]{2,1,0:T(2,128)(2,1)S(1)}, u32[]{:S(2)}, u32[]{:S(2)}) async-start(bf16[64,2,960]{2,1,0:T(2,128)(2,1)} %shard_map.140), calls=%async_computation | async-start | bytes 524288 | tf_op jit(solution)/shard_map/all_to_all | solution.py:251
  34.1 2.4 %collective-permute-start.1 = (bf16[384,576]{0,1:T(8,128)(2,1)S(1)}, bf16[384,576]{0,1:T(8,128)(2,1)S(1)}, u32[]{:S(2)}, u32[]{:S(2)}) collective-permute-start(bf16[384,576]{0,1:T(8,128)(2,1)S(1)} %copy-done.1), channel_id=1, source_target_pairs={{0,16},{16,0},{32,48},{48,32},{64,80},{80,64},{96,112},{112,96},{1... | collective-permute-start | bytes 1327112 | tf_op jit(solution)/shard_map/ppermute | solution.py:248
  36.5 2.0 %collective-permute-start.2 = (bf16[384,576]{0,1:T(8,128)(2,1)S(1)}, bf16[384,576]{0,1:T(8,128)(2,1)S(1)}, u32[]{:S(2)}, u32[]{:S(2)}) collective-permute-start(bf16[384,576]{0,1:T(8,128)(2,1)S(1)} %copy-done), channel_id=1, source_target_pairs={{0,16},{16,0},{32,48},{48,32},{64,80},{80,64},{96,112},{112,96},{1... | collective-permute-start | bytes 1327112 | tf_op jit(solution)/shard_map/ppermute | solution.py:249
  38.4 36.9 %all-to-all-done = bf16[64,2,960]{2,1,0:T(2,128)(2,1)S(1)} async-done(((bf16[64,2,960]{2,1,0:T(2,128)(2,1)}), bf16[64,2,960]{2,1,0:T(2,128)(2,1)S(1)}, u32[]{:S(2)}, u32[]{:S(2)}) %all-to-all-start) | async-done | bytes 245792 | tf_op jit(solution)/shard_map/all_to_all | solution.py:251
  75.5 3.3 %collective-permute-start = (bf16[128,384]{1,0:T(8,128)(2,1)S(1)}, bf16[128,384]{1,0:T(8,128)(2,1)S(1)}, u32[]{:S(2)}, u32[]{:S(2)}) collective-permute-start(bf16[128,384]{1,0:T(8,128)(2,1)S(1)} %slice.28), channel_id=1, source_target_pairs={{0,32},{16,48},{32,0},{48,16},{64,96},{80,112},{96,64},{112,80},{1... | collective-permute-start | bytes 294920 | tf_op jit(solution)/shard_map/ppermute | solution.py:256
  78.8 2.1 %collective-permute-done = bf16[128,384]{1,0:T(8,128)(2,1)S(1)} collective-permute-done((bf16[128,384]{1,0:T(8,128)(2,1)S(1)}, bf16[128,384]{1,0:T(8,128)(2,1)S(1)}, u32[]{:S(2)}, u32[]{:S(2)}) %collective-permute-start) | collective-permute-done | bytes 98336 | tf_op jit(solution)/shard_map/ppermute | solution.py:256
  80.9 0.8 convolution_convert_fusion
  81.7 21.4 %all_to_all.20 = bf16[16,16,2304]{2,1,0:T(8,128)(2,1)S(1)} all-to-all(bf16[16,16,2304]{2,1,0:T(8,128)(2,1)S(1)} %bitcast.6), channel_id=1, replica_groups=mesh['seq'=64,'head'=16] {'head'}, dimensions={0} | all-to-all | bytes 2359296 | tf_op jit(solution)/shard_map/all_to_all | solution.py:261
  103.3 0.9 broadcast_in_dim.2
  104.2 3.6 %all-to-all-start.2 = ((bf16[16,16,1152]{2,1,0:T(8,128)(2,1)}), bf16[16,16,1152]{2,1,0:T(8,128)(2,1)S(1)}, u32[]{:S(2)}, u32[]{:S(2)}) async-start(bf16[16,16,1152]{2,1,0:T(8,128)(2,1)} %broadcast_in_dim.2), calls=%async_computation.2 | async-start | bytes 1179648 | tf_op jit(solution)/shard_map/all_to_all | solution.py:278
  107.8 6.6 %collective-permute-start.3 = (bf16[576,384]{1,0:T(8,128)(2,1)S(1)}, bf16[576,384]{1,0:T(8,128)(2,1)S(1)}, u32[]{:S(2)}, u32[]{:S(2)}) collective-permute-start(bf16[576,384]{1,0:T(8,128)(2,1)S(1)} %copy-done.2), channel_id=1, source_target_pairs={{0,16},{16,0},{32,48},{48,32},{64,80},{80,64},{96,112},{112,96},{1... | collective-permute-start | bytes 1327112 | tf_op jit(solution)/shard_map/ppermute | solution.py:250
  114.4 1.4 collective-permute-done.3
  115.8 1.4 all-to-all-done.2
  117.7 4.3 %collective-permute-start.4 = (bf16[128,384]{1,0:T(8,128)(2,1)S(1)}, bf16[128,384]{1,0:T(8,128)(2,1)S(1)}, u32[]{:S(2)}, u32[]{:S(2)}) collective-permute-start(bf16[128,384]{1,0:T(8,128)(2,1)S(1)} %slice.32), channel_id=1, source_target_pairs={{0,32},{16,48},{32,0},{48,16},{64,96},{80,112},{96,64},{112,80},{1... | collective-permute-start | bytes 294920 | tf_op jit(solution)/shard_map/ppermute | solution.py:290
  122.6 0.7 slice.33.piece_ref
  123.2 2.1 %shard_map.141 = bf16[128,512]{1,0:T(8,128)(2,1)} custom-call(bf16[128,512]{1,0:T(8,128)(2,1)} %slice.33.piece_ref, bf16[128,64]{1,0:T(8,128)(2,1)} %slice.34.log_ref), custom_call_target="tpu_custom_call" | custom-call | flops 67108864 | bytes 262144 | tf_op jit(solution)/shard_map/pallas_call | solution.py:197
  125.4 0.9 pad_maximum_fusion
  126.3 0.8 reshape.26
  127.1 10.6 %all-to-all-start.3 = ((bf16[64,2,896]{2,1,0:T(2,128)(2,1)}), bf16[64,2,896]{2,1,0:T(2,128)(2,1)S(1)}, u32[]{:S(2)}, u32[]{:S(2)}) async-start(bf16[64,2,896]{2,1,0:T(2,128)(2,1)} %reshape.26), calls=%async_computation.3 | async-start | bytes 458752 | tf_op jit(solution)/shard_map/all_to_all | solution.py:293
  137.7 3.5 %shard_map.142 = (f32[256,512]{1,0:T(8,128)}, f32[256,512]{1,0:T(8,128)}, bf16[256,512]{1,0:T(8,128)(2,1)}, bf16[256,512]{1,0:T(8,128)(2,1)}, bf16[128,256]{1,0:T(8,128)(2,1)}, /*index=5*/bf16[128,256]{1,0:T(8,128)(2,1)}) custom-call(s32[4]{0:T(128)} %place_ref.3, bf16[256,512]{1,0:T(8,128)(2,1)} %query_ref.1, bf16[256,512]{1,0:T(8,128)(2,1)} %key_ref.3, ...), custom_call_target="tpu_custom_call" | custom-call | flops 536870912 | bytes 2097152 | tf_op jit(solution)/shard_map/pallas_call | solution.py:197
  141.2 35.4 %all-to-all-done.3 = bf16[64,2,896]{2,1,0:T(2,128)(2,1)S(1)} async-done(((bf16[64,2,896]{2,1,0:T(2,128)(2,1)}), bf16[64,2,896]{2,1,0:T(2,128)(2,1)S(1)}, u32[]{:S(2)}, u32[]{:S(2)}) %all-to-all-start.3) | async-done | bytes 229408 | tf_op jit(solution)/shard_map/all_to_all | solution.py:293
  176.6 0.8 reshape.27.back_ref
  177.3 2.7 %shard_map.143 = (bf16[256,512]{1,0:T(8,128)(2,1)}, bf16[256,384]{1,0:T(8,128)(2,1)}) custom-call(bf16[128,896]{1,0:T(8,128)(2,1)} %reshape.27.back_ref, f32[256,512]{1,0:T(8,128)} %get-tuple-element.8.intra_ref, f32[256,512]{1,0:T(8,128)} %get-tuple-element.9.factor_ref, bf16[256,512]{1,0:T(8,128)(2,1)} %get-tuple-element.10.high_ref, ...), custom_call_target="tpu_custom_call" | custom-call | flops 268435456 | bytes 1048576 | tf_op jit(solution)/shard_map/pallas_call | solution.py:197
  (17 shorter events, 1.5 us)
Async XLA Ops:
  0.6 33.5 %copy-start.1 = (bf16[384,576]{0,1:T(8,128)(2,1)S(1)}, bf16[384,576]{0,1:T(8,128)(2,1)}, u32[]{:S(2)}) copy-start(bf16[384,576]{0,1:T(8,128)(2,1)} %param.23) | copy-start | bytes 1327108
  0.6 35.8 %copy-start = (bf16[384,576]{0,1:T(8,128)(2,1)S(1)}, bf16[384,576]{0,1:T(8,128)(2,1)}, u32[]{:S(2)}) copy-start(bf16[384,576]{0,1:T(8,128)(2,1)} %param.24) | copy-start | bytes 1327108
  3.7 71.7 %all-to-all-start = ((bf16[64,2,960]{2,1,0:T(2,128)(2,1)}), bf16[64,2,960]{2,1,0:T(2,128)(2,1)S(1)}, u32[]{:S(2)}, u32[]{:S(2)}) async-start(bf16[64,2,960]{2,1,0:T(2,128)(2,1)} %shard_map.140), calls=%async_computation | async-start | bytes 524288 | tf_op jit(solution)/shard_map/all_to_all | solution.py:251
  34.1 44.7 %collective-permute-start.1 = (bf16[384,576]{0,1:T(8,128)(2,1)S(1)}, bf16[384,576]{0,1:T(8,128)(2,1)S(1)}, u32[]{:S(2)}, u32[]{:S(2)}) collective-permute-start(bf16[384,576]{0,1:T(8,128)(2,1)S(1)} %copy-done.1), channel_id=1, source_target_pairs={{0,16},{16,0},{32,48},{48,32},{64,80},{80,64},{96,112},{112,96},{1... | collective-permute-start | bytes 1327112 | tf_op jit(solution)/shard_map/ppermute | solution.py:248
  36.5 42.4 %collective-permute-start.2 = (bf16[384,576]{0,1:T(8,128)(2,1)S(1)}, bf16[384,576]{0,1:T(8,128)(2,1)S(1)}, u32[]{:S(2)}, u32[]{:S(2)}) collective-permute-start(bf16[384,576]{0,1:T(8,128)(2,1)S(1)} %copy-done), channel_id=1, source_target_pairs={{0,16},{16,0},{32,48},{48,32},{64,80},{80,64},{96,112},{112,96},{1... | collective-permute-start | bytes 1327112 | tf_op jit(solution)/shard_map/ppermute | solution.py:249
  75.5 5.4 %collective-permute-start = (bf16[128,384]{1,0:T(8,128)(2,1)S(1)}, bf16[128,384]{1,0:T(8,128)(2,1)S(1)}, u32[]{:S(2)}, u32[]{:S(2)}) collective-permute-start(bf16[128,384]{1,0:T(8,128)(2,1)S(1)} %slice.28), channel_id=1, source_target_pairs={{0,32},{16,48},{32,0},{48,16},{64,96},{80,112},{96,64},{112,80},{1... | collective-permute-start | bytes 294920 | tf_op jit(solution)/shard_map/ppermute | solution.py:256
  103.3 4.5 %copy-start.2 = (bf16[576,384]{1,0:T(8,128)(2,1)S(1)}, bf16[576,384]{1,0:T(8,128)(2,1)}, u32[]{:S(2)}) copy-start(bf16[576,384]{1,0:T(8,128)(2,1)} %param.25) | copy-start | bytes 1327108
  104.2 13.0 %all-to-all-start.2 = ((bf16[16,16,1152]{2,1,0:T(8,128)(2,1)}), bf16[16,16,1152]{2,1,0:T(8,128)(2,1)S(1)}, u32[]{:S(2)}, u32[]{:S(2)}) async-start(bf16[16,16,1152]{2,1,0:T(8,128)(2,1)} %broadcast_in_dim.2), calls=%async_computation.2 | async-start | bytes 1179648 | tf_op jit(solution)/shard_map/all_to_all | solution.py:278
  107.8 8.0 %collective-permute-start.3 = (bf16[576,384]{1,0:T(8,128)(2,1)S(1)}, bf16[576,384]{1,0:T(8,128)(2,1)S(1)}, u32[]{:S(2)}, u32[]{:S(2)}) collective-permute-start(bf16[576,384]{1,0:T(8,128)(2,1)S(1)} %copy-done.2), channel_id=1, source_target_pairs={{0,16},{16,0},{32,48},{48,32},{64,80},{80,64},{96,112},{112,96},{1... | collective-permute-start | bytes 1327112 | tf_op jit(solution)/shard_map/ppermute | solution.py:250
  117.7 7.7 %collective-permute-start.4 = (bf16[128,384]{1,0:T(8,128)(2,1)S(1)}, bf16[128,384]{1,0:T(8,128)(2,1)S(1)}, u32[]{:S(2)}, u32[]{:S(2)}) collective-permute-start(bf16[128,384]{1,0:T(8,128)(2,1)S(1)} %slice.32), channel_id=1, source_target_pairs={{0,32},{16,48},{32,0},{48,16},{64,96},{80,112},{96,64},{112,80},{1... | collective-permute-start | bytes 294920 | tf_op jit(solution)/shard_map/ppermute | solution.py:290
  127.1 49.5 %all-to-all-start.3 = ((bf16[64,2,896]{2,1,0:T(2,128)(2,1)}), bf16[64,2,896]{2,1,0:T(2,128)(2,1)S(1)}, u32[]{:S(2)}, u32[]{:S(2)}) async-start(bf16[64,2,896]{2,1,0:T(2,128)(2,1)} %reshape.26), calls=%async_computation.3 | async-start | bytes 458752 | tf_op jit(solution)/shard_map/all_to_all | solution.py:293

commit v5 on v4

--- a/solution.py
+++ b/solution.py
@@ -72,8 +72,8 @@
     for h in range(heads):
         cols = slice(h * width, (h + 1) * width)
         value = value_ref[:, cols]
-        high, low = two_parts(key_ref[:, cols].astype(jnp.float32) * jnp.exp(rest[:, h : h + 1]))
-        state = dot(high, value, TN) + dot(low, value, TN)
+        key = key_ref[:, cols].astype(jnp.float32) * jnp.exp(rest[:, h : h + 1])
+        state = dot(key.astype(jnp.bfloat16), value, TN)
         rows = slice(h * per_head // 2, (h + 1) * per_head // 2)
         for i in range(chunks):
             out_ref[rows, :, start + i * width : start + (i + 1) * width] = in_pairs(
@@ -90,8 +90,13 @@
     out_ref[:, :, stop : stop + 64] = in_pairs(jnp.where(lane < 3, parts, 0.0))
 
 
+def flat(x):
+    return x.astype(jnp.float32).reshape(2 * x.shape[0], x.shape[2]).astype(jnp.bfloat16)
+
+
 def scan_kernel(piece_ref, log_ref, out_ref):
-    n = out_ref.shape[0]
+    n = 2 * out_ref.shape[0]
+    feat = out_ref.shape[2] - piece_ref.shape[1]
     logs = jnp.sum(log_ref[:, 0:3].astype(jnp.float32), axis=1, keepdims=True)
     row, col = iota((n, n), 0), iota((n, n), 1)
     row_block, col_block = row >> 1, col >> 1
@@ -101,7 +106,8 @@
     used = (col_block < row_block) & ((col & 1) == (row & 1))
     high, low = two_parts(jnp.where(used, jnp.exp(spans), 0.0))
     pieces = piece_ref[...]
-    out_ref[...] = (dot(high, pieces, NN) + dot(low, pieces, NN)).astype(jnp.bfloat16)
+    out_ref[:, :, :feat] = jnp.zeros((n // 2, 2, feat), jnp.bfloat16)
+    out_ref[:, :, feat:] = in_pairs(dot(high, pieces, NN) + dot(low, pieces, NN))
 
 
 def side_kernel(
@@ -116,8 +122,7 @@
     route_ref,
     intra_ref,
     factor_ref,
-    high_ref,
-    low_ref,
+    scaled_ref,
     share_high_ref,
     share_low_ref,
 ):
@@ -138,7 +143,7 @@
         weights = jnp.where(lower, jnp.exp(jnp.where(lower, spread, 0.0)), 0.0)
         intra_ref[:, cols] = dot((scores * weights).astype(jnp.bfloat16), value_ref[:, cols], NN)
         scaled = query.astype(jnp.float32) * jnp.exp(cum_col[:, h : h + 1])
-        high_ref[:, cols], low_ref[:, cols] = two_parts(scaled)
+        scaled_ref[:, cols] = scaled.astype(jnp.bfloat16)
     factor_ref[...] = gain_ref[...] / (1.0 + jnp.exp(-gate_ref[...].astype(jnp.float32)))
     pick, first = picks(place_ref, ids_ref[...], block_rows, tokens)
     route = route_ref[...]
@@ -150,16 +155,15 @@
     back_ref,
     intra_ref,
     factor_ref,
-    high_ref,
-    low_ref,
+    scaled_ref,
     share_high_ref,
     share_low_ref,
     attention_ref,
     moe_ref,
 ):
-    block_rows = back_ref.shape[0]
+    block_rows = 2 * back_ref.shape[0]
     feat = moe_ref.shape[1]
-    pieces = back_ref[:, :feat]
+    pieces = flat(back_ref[:, :, :feat])
     total = dot(share_high_ref[...], pieces, TN) + dot(share_low_ref[...], pieces, TN)
     moe_ref[...] = total.astype(jnp.bfloat16)
     width = 128
@@ -168,19 +172,15 @@
     chunks = width // per_head
     for h in range(heads):
         cols = slice(h * width, (h + 1) * width)
-        rows = slice(h * per_head, (h + 1) * per_head)
+        rows = slice(h * per_head // 2, (h + 1) * per_head // 2)
         state = jnp.concatenate(
             [
-                back_ref[rows, feat + i * width : feat + (i + 1) * width]
+                flat(back_ref[rows, :, feat + i * width : feat + (i + 1) * width])
                 for i in range(chunks)
             ],
             axis=0,
         )
-        mixed = (
-            intra_ref[:, cols]
-            + dot(high_ref[:, cols], state, NN)
-            + dot(low_ref[:, cols], state, NN)
-        )
+        mixed = intra_ref[:, cols] + dot(scaled_ref[:, cols], state, NN)
         power = jnp.sum(mixed * mixed, axis=1, keepdims=True) * (1.0 / width)
         attention_ref[:, cols] = (mixed * lax.rsqrt(power + norm_eps) * factor_ref[:, cols]).astype(
             jnp.bfloat16
@@ -267,7 +267,7 @@
     )
     prefix_piece = call(
         scan_kernel,
-        [((lines, state_len), bf16)],
+        [((seq_count, 2, feat + state_len), bf16)],
         0,
         2**26,
         arrived[:, feat : feat + state_len],
@@ -289,16 +289,17 @@
     ).astype(bf16)
     near_piece = lax.ppermute(piece[lines:], "seq", next_chip)
     piece = (piece[:lines].astype(f32) + near_piece.astype(f32)).astype(bf16)
-    leaving = jnp.concatenate([piece, prefix_piece], axis=1)
+    leaving = lax.dynamic_update_slice(
+        prefix_piece, piece.reshape(seq_count, 2, feat), (0, 0, 0)
+    )
     returned = lax.all_to_all(
-        leaving.reshape(seq_count, 2, -1), "seq", split_axis=0, concat_axis=0, tiled=True
-    ).reshape(lines, -1)
+        leaving, "seq", split_axis=0, concat_axis=0, tiled=True
+    )
     side = call(
         side_kernel,
         [
             ((tokens, heads_here * width), f32),
             ((tokens, heads_here * width), f32),
-            ((tokens, heads_here * width), bf16),
             ((tokens, heads_here * width), bf16),
             ((lines, tokens), bf16),
             ((lines, tokens), bf16),

time: 181 us -> 179 us (0.989)
  no operation moved by 1% of the time
where the time goes in v5:
time: 179 us
  waiting for transfers between devices  77.2 us (43%)
  starting transfers between devices  63.1 us (35%)
  blocking collectives  21.4 us (12%)
  Pallas kernels  11.1 us (6%)
  local copies, waits for them, and re-layouts  3.78 us (2%)
    all_to_all x1, waiting for transfers between devices, per_device(): lax.all_to_all(outgoing, 'seq', split_axis=0, concat_axis=0, tiled=True)  36.9 us
    all_to_all x1, waiting for transfers between devices, per_device(): lax.all_to_all(leaving, 'seq', split_axis=0, concat_axis=0, tiled=True)  35.4 us
    all_to_all x1, starting transfers between devices, per_device(): lax.all_to_all(outgoing, 'seq', split_axis=0, concat_axis=0, tiled=True)  30.4 us
    all_to_all x1, blocking collectives, per_device(): lax.all_to_all(gate_up.reshape(head_count, rows // head_count, 4 * ff), '...  21.4 us
    pallas_call x4, Pallas kernels, call(): pl.pallas_call(kernel, in_specs=specs, out_specs=out_specs, out_shape=out...  11.1 us
    all_to_all x1, starting transfers between devices, per_device(): lax.all_to_all(leaving, 'seq', split_axis=0, concat_axis=0, tiled=True)  10.6 us
    ppermute x1, starting transfers between devices, per_device(): other_down = lax.ppermute(down_weight, 'seq', swap)  6.62 us
    ppermute x1, starting transfers between devices, per_device(): near_piece = lax.ppermute(piece[lines:], 'seq', next_chip)  4.26 us
  transfers between devices with their start and end apart: 8, of which 5 were waited for; matrix products, arithmetic and copies ran while one was open for 1% of the time, Pallas kernels for 3%

profile of v5, /device:TPU:1, one launch (start us, length us, event | category | flops | bytes accessed | tf_op | source)
XLA Modules:
  0.0 178.8 jit_solution(6903431453826042368)
XLA Ops:
  0.7 2.9 %shard_map.140 = bf16[64,2,960]{2,1,0:T(2,128)(2,1)} custom-call(s32[4]{0:T(128)} %place_ref.3, bf16[256,512]{1,0:T(8,128)(2,1)} %key_ref.3, bf16[256,512]{1,0:T(8,128)(2,1)} %value_ref.3, f32[4,256]{1,0:T(4,128)} %decay_ref.3, bf16[256,384]{1,0:T(8,128)(2,1)} %feat_ref.1, s32[2,256]{1,0:T(2,128)} %bitcast.8), custom_call_target="tpu_custom_call" | custom-call | flops 268435456 | bytes 1048576 | tf_op jit(solution)/shard_map/pallas_call | solution.py:197
  3.5 30.4 %all-to-all-start = ((bf16[64,2,960]{2,1,0:T(2,128)(2,1)}), bf16[64,2,960]{2,1,0:T(2,128)(2,1)S(1)}, u32[]{:S(2)}, u32[]{:S(2)}) async-start(bf16[64,2,960]{2,1,0:T(2,128)(2,1)} %shard_map.140), calls=%async_computation | async-start | bytes 524288 | tf_op jit(solution)/shard_map/all_to_all | solution.py:251
  33.9 2.4 %collective-permute-start.1 = (bf16[384,576]{0,1:T(8,128)(2,1)S(1)}, bf16[384,576]{0,1:T(8,128)(2,1)S(1)}, u32[]{:S(2)}, u32[]{:S(2)}) collective-permute-start(bf16[384,576]{0,1:T(8,128)(2,1)S(1)} %copy-done.2), channel_id=1, source_target_pairs={{0,16},{16,0},{32,48},{48,32},{64,80},{80,64},{96,112},{112,96},{1... | collective-permute-start | bytes 1327112 | tf_op jit(solution)/shard_map/ppermute | solution.py:248
  36.3 2.0 %collective-permute-start.2 = (bf16[384,576]{0,1:T(8,128)(2,1)S(1)}, bf16[384,576]{0,1:T(8,128)(2,1)S(1)}, u32[]{:S(2)}, u32[]{:S(2)}) collective-permute-start(bf16[384,576]{0,1:T(8,128)(2,1)S(1)} %copy-done.1), channel_id=1, source_target_pairs={{0,16},{16,0},{32,48},{48,32},{64,80},{80,64},{96,112},{112,96},{1... | collective-permute-start | bytes 1327112 | tf_op jit(solution)/shard_map/ppermute | solution.py:249
  38.3 36.9 %all-to-all-done = bf16[64,2,960]{2,1,0:T(2,128)(2,1)S(1)} async-done(((bf16[64,2,960]{2,1,0:T(2,128)(2,1)}), bf16[64,2,960]{2,1,0:T(2,128)(2,1)S(1)}, u32[]{:S(2)}, u32[]{:S(2)}) %all-to-all-start) | async-done | bytes 245792 | tf_op jit(solution)/shard_map/all_to_all | solution.py:251
  75.4 3.3 %collective-permute-start = (bf16[128,384]{1,0:T(8,128)(2,1)S(1)}, bf16[128,384]{1,0:T(8,128)(2,1)S(1)}, u32[]{:S(2)}, u32[]{:S(2)}) collective-permute-start(bf16[128,384]{1,0:T(8,128)(2,1)S(1)} %slice.30), channel_id=1, source_target_pairs={{0,32},{16,48},{32,0},{48,16},{64,96},{80,112},{96,64},{112,80},{1... | collective-permute-start | bytes 294920 | tf_op jit(solution)/shard_map/ppermute | solution.py:256
  78.7 2.1 %collective-permute-done = bf16[128,384]{1,0:T(8,128)(2,1)S(1)} collective-permute-done((bf16[128,384]{1,0:T(8,128)(2,1)S(1)}, bf16[128,384]{1,0:T(8,128)(2,1)S(1)}, u32[]{:S(2)}, u32[]{:S(2)}) %collective-permute-start) | collective-permute-done | bytes 98336 | tf_op jit(solution)/shard_map/ppermute | solution.py:256
  80.8 0.8 convolution_convert_fusion
  81.6 21.4 %all_to_all.20 = bf16[16,16,2304]{2,1,0:T(8,128)(2,1)S(1)} all-to-all(bf16[16,16,2304]{2,1,0:T(8,128)(2,1)S(1)} %bitcast.6), channel_id=1, replica_groups=mesh['seq'=64,'head'=16] {'head'}, dimensions={0} | all-to-all | bytes 2359296 | tf_op jit(solution)/shard_map/all_to_all | solution.py:261
  103.2 0.9 broadcast_in_dim.2
  104.0 3.6 %all-to-all-start.2 = ((bf16[16,16,1152]{2,1,0:T(8,128)(2,1)}), bf16[16,16,1152]{2,1,0:T(8,128)(2,1)S(1)}, u32[]{:S(2)}, u32[]{:S(2)}) async-start(bf16[16,16,1152]{2,1,0:T(8,128)(2,1)} %broadcast_in_dim.2), calls=%async_computation.2 | async-start | bytes 1179648 | tf_op jit(solution)/shard_map/all_to_all | solution.py:278
  107.6 6.6 %collective-permute-start.3 = (bf16[576,384]{1,0:T(8,128)(2,1)S(1)}, bf16[576,384]{1,0:T(8,128)(2,1)S(1)}, u32[]{:S(2)}, u32[]{:S(2)}) collective-permute-start(bf16[576,384]{1,0:T(8,128)(2,1)S(1)} %copy-done.3), channel_id=1, source_target_pairs={{0,16},{16,0},{32,48},{48,32},{64,80},{80,64},{96,112},{112,96},{1... | collective-permute-start | bytes 1327112 | tf_op jit(solution)/shard_map/ppermute | solution.py:250
  114.3 1.4 collective-permute-done.3
  115.7 1.4 all-to-all-done.2
  117.5 4.3 %collective-permute-start.4 = (bf16[128,384]{1,0:T(8,128)(2,1)S(1)}, bf16[128,384]{1,0:T(8,128)(2,1)S(1)}, u32[]{:S(2)}, u32[]{:S(2)}) collective-permute-start(bf16[128,384]{1,0:T(8,128)(2,1)S(1)} %slice.34), channel_id=1, source_target_pairs={{0,32},{16,48},{32,0},{48,16},{64,96},{80,112},{96,64},{112,80},{1... | collective-permute-start | bytes 294920 | tf_op jit(solution)/shard_map/ppermute | solution.py:290
  121.8 0.6 slice.29.log_ref
  122.4 0.7 slice.28.piece_ref
  123.1 2.2 %shard_map.141 = bf16[64,2,896]{2,1,0:T(2,128)(2,1)} custom-call(bf16[128,512]{1,0:T(8,128)(2,1)} %slice.28.piece_ref, bf16[128,64]{1,0:T(8,128)(2,1)} %slice.29.log_ref), custom_call_target="tpu_custom_call" | custom-call | flops 67108864 | bytes 262144 | tf_op jit(solution)/shard_map/pallas_call | solution.py:197
  125.4 0.7 constant_dynamic-update-slice_fusion
  126.1 10.6 %all-to-all-start.3 = ((bf16[64,2,896]{2,1,0:T(2,128)(2,1)}), bf16[64,2,896]{2,1,0:T(2,128)(2,1)S(1)}, u32[]{:S(2)}, u32[]{:S(2)}) async-start(bf16[64,2,896]{2,1,0:T(2,128)(2,1)} %constant_dynamic-update-slice_fusion), calls=%async_computation.3 | async-start | bytes 458752 | tf_op jit(solution)/shard_map/all_to_all | solution.py:295
  136.7 3.4 %shard_map.142 = (f32[256,512]{1,0:T(8,128)}, f32[256,512]{1,0:T(8,128)}, bf16[256,512]{1,0:T(8,128)(2,1)}, bf16[128,256]{1,0:T(8,128)(2,1)}, bf16[128,256]{1,0:T(8,128)(2,1)}) custom-call(s32[4]{0:T(128)} %place_ref.3, bf16[256,512]{1,0:T(8,128)(2,1)} %query_ref.1, bf16[256,512]{1,0:T(8,128)(2,1)} %key_ref.3, bf16[256,512]{1,0:T(8,128)(2,1)} %value_ref.3, ...), custom_call_target="tpu_custom_call" | custom-call | flops 536870912 | bytes 2097152 | tf_op jit(solution)/shard_map/pallas_call | solution.py:197
  140.1 35.4 %all-to-all-done.3.back_ref = bf16[64,2,896]{2,1,0:T(2,128)(2,1)S(1)} async-done(((bf16[64,2,896]{2,1,0:T(2,128)(2,1)}), bf16[64,2,896]{2,1,0:T(2,128)(2,1)S(1)}, u32[]{:S(2)}, u32[]{:S(2)}) %all-to-all-start.3) | async-done | bytes 229408 | tf_op jit(solution)/shard_map/all_to_all | solution.py:295
  175.5 0.7 copy-done
  176.2 2.5 %shard_map.143 = (bf16[256,512]{1,0:T(8,128)(2,1)}, bf16[256,384]{1,0:T(8,128)(2,1)}) custom-call(bf16[64,2,896]{2,1,0:T(2,128)(2,1)} %copy-done, f32[256,512]{1,0:T(8,128)} %get-tuple-element.7.intra_ref, f32[256,512]{1,0:T(8,128)} %get-tuple-element.8.factor_ref, bf16[256,512]{1,0:T(8,128)(2,1)} %get-tuple-element.9.scaled_ref, ...), custom_call_target="tpu_custom_call" | custom-call | flops 268435456 | bytes 1048576 | tf_op jit(solution)/shard_map/pallas_call | solution.py:197
  (18 shorter events, 0.9 us)
Async XLA Ops:
  0.6 33.3 %copy-start.2 = (bf16[384,576]{0,1:T(8,128)(2,1)S(1)}, bf16[384,576]{0,1:T(8,128)(2,1)}, u32[]{:S(2)}) copy-start(bf16[384,576]{0,1:T(8,128)(2,1)} %param.23) | copy-start | bytes 1327108
  0.6 35.7 %copy-start.1 = (bf16[384,576]{0,1:T(8,128)(2,1)S(1)}, bf16[384,576]{0,1:T(8,128)(2,1)}, u32[]{:S(2)}) copy-start(bf16[384,576]{0,1:T(8,128)(2,1)} %param.24) | copy-start | bytes 1327108
  3.5 71.7 %all-to-all-start = ((bf16[64,2,960]{2,1,0:T(2,128)(2,1)}), bf16[64,2,960]{2,1,0:T(2,128)(2,1)S(1)}, u32[]{:S(2)}, u32[]{:S(2)}) async-start(bf16[64,2,960]{2,1,0:T(2,128)(2,1)} %shard_map.140), calls=%async_computation | async-start | bytes 524288 | tf_op jit(solution)/shard_map/all_to_all | solution.py:251
  33.9 44.7 %collective-permute-start.1 = (bf16[384,576]{0,1:T(8,128)(2,1)S(1)}, bf16[384,576]{0,1:T(8,128)(2,1)S(1)}, u32[]{:S(2)}, u32[]{:S(2)}) collective-permute-start(bf16[384,576]{0,1:T(8,128)(2,1)S(1)} %copy-done.2), channel_id=1, source_target_pairs={{0,16},{16,0},{32,48},{48,32},{64,80},{80,64},{96,112},{112,96},{1... | collective-permute-start | bytes 1327112 | tf_op jit(solution)/shard_map/ppermute | solution.py:248
  36.3 42.4 %collective-permute-start.2 = (bf16[384,576]{0,1:T(8,128)(2,1)S(1)}, bf16[384,576]{0,1:T(8,128)(2,1)S(1)}, u32[]{:S(2)}, u32[]{:S(2)}) collective-permute-start(bf16[384,576]{0,1:T(8,128)(2,1)S(1)} %copy-done.1), channel_id=1, source_target_pairs={{0,16},{16,0},{32,48},{48,32},{64,80},{80,64},{96,112},{112,96},{1... | collective-permute-start | bytes 1327112 | tf_op jit(solution)/shard_map/ppermute | solution.py:249
  75.4 5.4 %collective-permute-start = (bf16[128,384]{1,0:T(8,128)(2,1)S(1)}, bf16[128,384]{1,0:T(8,128)(2,1)S(1)}, u32[]{:S(2)}, u32[]{:S(2)}) collective-permute-start(bf16[128,384]{1,0:T(8,128)(2,1)S(1)} %slice.30), channel_id=1, source_target_pairs={{0,32},{16,48},{32,0},{48,16},{64,96},{80,112},{96,64},{112,80},{1... | collective-permute-start | bytes 294920 | tf_op jit(solution)/shard_map/ppermute | solution.py:256
  103.1 4.5 %copy-start.3 = (bf16[576,384]{1,0:T(8,128)(2,1)S(1)}, bf16[576,384]{1,0:T(8,128)(2,1)}, u32[]{:S(2)}) copy-start(bf16[576,384]{1,0:T(8,128)(2,1)} %param.25) | copy-start | bytes 1327108
  104.0 13.0 %all-to-all-start.2 = ((bf16[16,16,1152]{2,1,0:T(8,128)(2,1)}), bf16[16,16,1152]{2,1,0:T(8,128)(2,1)S(1)}, u32[]{:S(2)}, u32[]{:S(2)}) async-start(bf16[16,16,1152]{2,1,0:T(8,128)(2,1)} %broadcast_in_dim.2), calls=%async_computation.2 | async-start | bytes 1179648 | tf_op jit(solution)/shard_map/all_to_all | solution.py:278
  107.6 8.0 %collective-permute-start.3 = (bf16[576,384]{1,0:T(8,128)(2,1)S(1)}, bf16[576,384]{1,0:T(8,128)(2,1)S(1)}, u32[]{:S(2)}, u32[]{:S(2)}) collective-permute-start(bf16[576,384]{1,0:T(8,128)(2,1)S(1)} %copy-done.3), channel_id=1, source_target_pairs={{0,16},{16,0},{32,48},{48,32},{64,80},{80,64},{96,112},{112,96},{1... | collective-permute-start | bytes 1327112 | tf_op jit(solution)/shard_map/ppermute | solution.py:250
  117.5 7.8 %collective-permute-start.4 = (bf16[128,384]{1,0:T(8,128)(2,1)S(1)}, bf16[128,384]{1,0:T(8,128)(2,1)S(1)}, u32[]{:S(2)}, u32[]{:S(2)}) collective-permute-start(bf16[128,384]{1,0:T(8,128)(2,1)S(1)} %slice.34), channel_id=1, source_target_pairs={{0,32},{16,48},{32,0},{48,16},{64,96},{80,112},{96,64},{112,80},{1... | collective-permute-start | bytes 294920 | tf_op jit(solution)/shard_map/ppermute | solution.py:290
  126.1 49.4 %all-to-all-start.3 = ((bf16[64,2,896]{2,1,0:T(2,128)(2,1)}), bf16[64,2,896]{2,1,0:T(2,128)(2,1)S(1)}, u32[]{:S(2)}, u32[]{:S(2)}) async-start(bf16[64,2,896]{2,1,0:T(2,128)(2,1)} %constant_dynamic-update-slice_fusion), calls=%async_computation.3 | async-start | bytes 458752 | tf_op jit(solution)/shard_map/all_to_all | solution.py:295
  175.5 0.7 copy-start

commit v6 on v5

--- a/solution.py
+++ b/solution.py
@@ -94,10 +94,14 @@
     return x.astype(jnp.float32).reshape(2 * x.shape[0], x.shape[2]).astype(jnp.bfloat16)
 
 
-def scan_kernel(piece_ref, log_ref, out_ref):
+STATE = 4 * 128 * 128
+
+
+def scan_kernel(arrived_ref, out_ref):
     n = 2 * out_ref.shape[0]
-    feat = out_ref.shape[2] - piece_ref.shape[1]
-    logs = jnp.sum(log_ref[:, 0:3].astype(jnp.float32), axis=1, keepdims=True)
+    end = out_ref.shape[2]
+    feat = end - STATE // n
+    logs = jnp.sum(arrived_ref[:, end : end + 3].astype(jnp.float32), axis=1, keepdims=True)
     row, col = iota((n, n), 0), iota((n, n), 1)
     row_block, col_block = row >> 1, col >> 1
     before = jnp.where((col_block < row_block) & ((col & 1) == 0), 1.0, 0.0)
@@ -105,7 +109,7 @@
     spans = dot(before, later, NN, HIGHEST)
     used = (col_block < row_block) & ((col & 1) == (row & 1))
     high, low = two_parts(jnp.where(used, jnp.exp(spans), 0.0))
-    pieces = piece_ref[...]
+    pieces = arrived_ref[:, feat:end]
     out_ref[:, :, :feat] = jnp.zeros((n // 2, 2, feat), jnp.bfloat16)
     out_ref[:, :, feat:] = in_pairs(dot(high, pieces, NN) + dot(low, pieces, NN))
 
@@ -265,14 +269,7 @@
         concat_axis=0,
         tiled=True,
     )
-    prefix_piece = call(
-        scan_kernel,
-        [((seq_count, 2, feat + state_len), bf16)],
-        0,
-        2**26,
-        arrived[:, feat : feat + state_len],
-        arrived[:, feat + state_len :],
-    )
+    prefix_piece = call(scan_kernel, [((seq_count, 2, feat + state_len), bf16)], 0, 2**26, arrived)
     summed = jnp.sum(parts.astype(f32), axis=0)
     hidden_part = (jax.nn.silu(summed[:, : 2 * ff]) * summed[:, 2 * ff :]).astype(bf16)
     hidden = lax.all_to_all(

time: 179 us -> 179 us (level)
  transfers between devices with their start and end apart: 8 -> 8, of which waited for: 5 -> 5; matrix products, arithmetic and copies ran while one was open for 1% -> 0% of each run, Pallas kernels for 3% -> 3%
where the time goes in v6:
time: 179 us; the launch traced here: 178 us
  waiting for transfers between devices  77.2 us (43%)
  starting transfers between devices  63.9 us (36%)
  blocking collectives  21.4 us (12%)
  Pallas kernels  11.1 us (6%)
  local copies, waits for them, and re-layouts  2.52 us (1%)
    all_to_all x1, waiting for transfers between devices, per_device(): lax.all_to_all(outgoing, 'seq', split_axis=0, concat_axis=0, tiled=True)  36.9 us
    all_to_all x1, waiting for transfers between devices, per_device(): lax.all_to_all(leaving, 'seq', split_axis=0, concat_axis=0, tiled=True)  35.4 us
    all_to_all x1, starting transfers between devices, per_device(): lax.all_to_all(outgoing, 'seq', split_axis=0, concat_axis=0, tiled=True)  30.4 us
    all_to_all x1, blocking collectives, per_device(): lax.all_to_all(gate_up.reshape(head_count, rows // head_count, 4 * ff), '...  21.4 us
    all_to_all x1, starting transfers between devices, per_device(): lax.all_to_all(leaving, 'seq', split_axis=0, concat_axis=0, tiled=True)  11.5 us
    pallas_call x4, Pallas kernels, call(): pl.pallas_call(kernel, in_specs=specs, out_specs=out_specs, out_shape=out...  11.1 us
    ppermute x1, starting transfers between devices, per_device(): other_down = lax.ppermute(down_weight, 'seq', swap)  6.63 us
    ppermute x1, starting transfers between devices, per_device(): near_piece = lax.ppermute(piece[lines:], 'seq', next_chip)  4.25 us
  transfers between devices with their start and end apart: 8, of which 5 were waited for; matrix products, arithmetic and copies ran while one was open for 0% of the time, Pallas kernels for 3%

profile of v6, /device:TPU:1, one launch (start us, length us, event | category | flops | bytes accessed | tf_op | source)
XLA Modules:
  0.0 178.4 jit_solution(9146034809997029643)
XLA Ops:
  0.7 2.9 %shard_map.140 = bf16[64,2,960]{2,1,0:T(2,128)(2,1)} custom-call(s32[4]{0:T(128)} %place_ref.3, bf16[256,512]{1,0:T(8,128)(2,1)} %key_ref.3, bf16[256,512]{1,0:T(8,128)(2,1)} %value_ref.3, f32[4,256]{1,0:T(4,128)} %decay_ref.3, bf16[256,384]{1,0:T(8,128)(2,1)} %feat_ref.1, s32[2,256]{1,0:T(2,128)} %bitcast.8), custom_call_target="tpu_custom_call" | custom-call | flops 268435456 | bytes 1048576 | tf_op jit(solution)/shard_map/pallas_call | solution.py:201
  3.5 30.4 %all-to-all-start = ((bf16[64,2,960]{2,1,0:T(2,128)(2,1)}), bf16[64,2,960]{2,1,0:T(2,128)(2,1)S(1)}, u32[]{:S(2)}, u32[]{:S(2)}) async-start(bf16[64,2,960]{2,1,0:T(2,128)(2,1)} %shard_map.140), calls=%async_computation | async-start | bytes 524288 | tf_op jit(solution)/shard_map/all_to_all | solution.py:255
  33.9 2.4 %collective-permute-start.1 = (bf16[384,576]{0,1:T(8,128)(2,1)S(1)}, bf16[384,576]{0,1:T(8,128)(2,1)S(1)}, u32[]{:S(2)}, u32[]{:S(2)}) collective-permute-start(bf16[384,576]{0,1:T(8,128)(2,1)S(1)} %copy-done.3), channel_id=1, source_target_pairs={{0,16},{16,0},{32,48},{48,32},{64,80},{80,64},{96,112},{112,96},{1... | collective-permute-start | bytes 1327112 | tf_op jit(solution)/shard_map/ppermute | solution.py:252
  36.3 2.0 %collective-permute-start.2 = (bf16[384,576]{0,1:T(8,128)(2,1)S(1)}, bf16[384,576]{0,1:T(8,128)(2,1)S(1)}, u32[]{:S(2)}, u32[]{:S(2)}) collective-permute-start(bf16[384,576]{0,1:T(8,128)(2,1)S(1)} %copy-done.2), channel_id=1, source_target_pairs={{0,16},{16,0},{32,48},{48,32},{64,80},{80,64},{96,112},{112,96},{1... | collective-permute-start | bytes 1327112 | tf_op jit(solution)/shard_map/ppermute | solution.py:253
  38.3 36.9 %all-to-all-done = bf16[64,2,960]{2,1,0:T(2,128)(2,1)S(1)} async-done(((bf16[64,2,960]{2,1,0:T(2,128)(2,1)}), bf16[64,2,960]{2,1,0:T(2,128)(2,1)S(1)}, u32[]{:S(2)}, u32[]{:S(2)}) %all-to-all-start) | async-done | bytes 245792 | tf_op jit(solution)/shard_map/all_to_all | solution.py:255
  75.2 0.2 reshape.20.arrived_ref
  75.4 3.3 %collective-permute-start = (bf16[128,384]{1,0:T(8,128)(2,1)S(1)}, bf16[128,384]{1,0:T(8,128)(2,1)S(1)}, u32[]{:S(2)}, u32[]{:S(2)}) collective-permute-start(bf16[128,384]{1,0:T(8,128)(2,1)S(1)} %slice.20), channel_id=1, source_target_pairs={{0,32},{16,48},{32,0},{48,16},{64,96},{80,112},{96,64},{112,80},{1... | collective-permute-start | bytes 294920 | tf_op jit(solution)/shard_map/ppermute | solution.py:260
  78.7 2.1 %collective-permute-done = bf16[128,384]{1,0:T(8,128)(2,1)S(1)} collective-permute-done((bf16[128,384]{1,0:T(8,128)(2,1)S(1)}, bf16[128,384]{1,0:T(8,128)(2,1)S(1)}, u32[]{:S(2)}, u32[]{:S(2)}) %collective-permute-start) | collective-permute-done | bytes 98336 | tf_op jit(solution)/shard_map/ppermute | solution.py:260
  80.8 0.8 convolution_convert_fusion
  81.6 21.4 %all_to_all.20 = bf16[16,16,2304]{2,1,0:T(8,128)(2,1)S(1)} all-to-all(bf16[16,16,2304]{2,1,0:T(8,128)(2,1)S(1)} %bitcast.6), channel_id=1, replica_groups=mesh['seq'=64,'head'=16] {'head'}, dimensions={0} | all-to-all | bytes 2359296 | tf_op jit(solution)/shard_map/all_to_all | solution.py:265
  103.2 0.9 broadcast_in_dim.2
  104.1 3.6 %all-to-all-start.2 = ((bf16[16,16,1152]{2,1,0:T(8,128)(2,1)}), bf16[16,16,1152]{2,1,0:T(8,128)(2,1)S(1)}, u32[]{:S(2)}, u32[]{:S(2)}) async-start(bf16[16,16,1152]{2,1,0:T(8,128)(2,1)} %broadcast_in_dim.2), calls=%async_computation.2 | async-start | bytes 1179648 | tf_op jit(solution)/shard_map/all_to_all | solution.py:275
  107.7 6.6 %collective-permute-start.3 = (bf16[576,384]{1,0:T(8,128)(2,1)S(1)}, bf16[576,384]{1,0:T(8,128)(2,1)S(1)}, u32[]{:S(2)}, u32[]{:S(2)}) collective-permute-start(bf16[576,384]{1,0:T(8,128)(2,1)S(1)} %copy-done.4), channel_id=1, source_target_pairs={{0,16},{16,0},{32,48},{48,32},{64,80},{80,64},{96,112},{112,96},{1... | collective-permute-start | bytes 1327112 | tf_op jit(solution)/shard_map/ppermute | solution.py:254
  114.3 1.4 collective-permute-done.3
  115.7 1.4 all-to-all-done.2
  117.1 0.5 convolution_convert_fusion.1
  117.6 4.3 %collective-permute-start.4 = (bf16[128,384]{1,0:T(8,128)(2,1)S(1)}, bf16[128,384]{1,0:T(8,128)(2,1)S(1)}, u32[]{:S(2)}, u32[]{:S(2)}) collective-permute-start(bf16[128,384]{1,0:T(8,128)(2,1)S(1)} %slice.24), channel_id=1, source_target_pairs={{0,32},{16,48},{32,0},{48,16},{64,96},{80,112},{96,64},{112,80},{1... | collective-permute-start | bytes 294920 | tf_op jit(solution)/shard_map/ppermute | solution.py:287
  121.8 2.3 %shard_map.141 = bf16[64,2,896]{2,1,0:T(2,128)(2,1)} custom-call(bf16[128,960]{1,0:T(8,128)(2,1)} %copy-done), custom_call_target="tpu_custom_call" | custom-call | flops 67108864 | bytes 262144 | tf_op jit(solution)/shard_map/pallas_call | solution.py:201
  124.2 0.7 constant_dynamic-update-slice_fusion
  124.9 11.5 %all-to-all-start.3 = ((bf16[64,2,896]{2,1,0:T(2,128)(2,1)}), bf16[64,2,896]{2,1,0:T(2,128)(2,1)S(1)}, u32[]{:S(2)}, u32[]{:S(2)}) async-start(bf16[64,2,896]{2,1,0:T(2,128)(2,1)} %constant_dynamic-update-slice_fusion), calls=%async_computation.3 | async-start | bytes 458752 | tf_op jit(solution)/shard_map/all_to_all | solution.py:292
  136.4 3.4 %shard_map.142 = (f32[256,512]{1,0:T(8,128)}, f32[256,512]{1,0:T(8,128)}, bf16[256,512]{1,0:T(8,128)(2,1)}, bf16[128,256]{1,0:T(8,128)(2,1)}, bf16[128,256]{1,0:T(8,128)(2,1)}) custom-call(s32[4]{0:T(128)} %place_ref.3, bf16[256,512]{1,0:T(8,128)(2,1)} %query_ref.1, bf16[256,512]{1,0:T(8,128)(2,1)} %key_ref.3, bf16[256,512]{1,0:T(8,128)(2,1)} %value_ref.3, ...), custom_call_target="tpu_custom_call" | custom-call | flops 536870912 | bytes 2097152 | tf_op jit(solution)/shard_map/pallas_call | solution.py:201
  139.8 35.4 %all-to-all-done.3.back_ref = bf16[64,2,896]{2,1,0:T(2,128)(2,1)S(1)} async-done(((bf16[64,2,896]{2,1,0:T(2,128)(2,1)}), bf16[64,2,896]{2,1,0:T(2,128)(2,1)S(1)}, u32[]{:S(2)}, u32[]{:S(2)}) %all-to-all-start.3) | async-done | bytes 229408 | tf_op jit(solution)/shard_map/all_to_all | solution.py:292
  175.2 0.7 copy-done.1
  175.9 2.5 %shard_map.143 = (bf16[256,512]{1,0:T(8,128)(2,1)}, bf16[256,384]{1,0:T(8,128)(2,1)}) custom-call(bf16[64,2,896]{2,1,0:T(2,128)(2,1)} %copy-done.1, f32[256,512]{1,0:T(8,128)} %get-tuple-element.7.intra_ref, f32[256,512]{1,0:T(8,128)} %get-tuple-element.8.factor_ref, bf16[256,512]{1,0:T(8,128)(2,1)} %get-tuple-element.9.scaled_ref, ...), custom_call_target="tpu_custom_call" | custom-call | flops 268435456 | bytes 1048576 | tf_op jit(solution)/shard_map/pallas_call | solution.py:201
  (18 shorter events, 0.3 us)
Async XLA Ops:
  0.6 33.3 %copy-start.3 = (bf16[384,576]{0,1:T(8,128)(2,1)S(1)}, bf16[384,576]{0,1:T(8,128)(2,1)}, u32[]{:S(2)}) copy-start(bf16[384,576]{0,1:T(8,128)(2,1)} %param.23) | copy-start | bytes 1327108
  0.6 35.7 %copy-start.2 = (bf16[384,576]{0,1:T(8,128)(2,1)S(1)}, bf16[384,576]{0,1:T(8,128)(2,1)}, u32[]{:S(2)}) copy-start(bf16[384,576]{0,1:T(8,128)(2,1)} %param.24) | copy-start | bytes 1327108
  3.5 71.7 %all-to-all-start = ((bf16[64,2,960]{2,1,0:T(2,128)(2,1)}), bf16[64,2,960]{2,1,0:T(2,128)(2,1)S(1)}, u32[]{:S(2)}, u32[]{:S(2)}) async-start(bf16[64,2,960]{2,1,0:T(2,128)(2,1)} %shard_map.140), calls=%async_computation | async-start | bytes 524288 | tf_op jit(solution)/shard_map/all_to_all | solution.py:255
  33.9 44.8 %collective-permute-start.1 = (bf16[384,576]{0,1:T(8,128)(2,1)S(1)}, bf16[384,576]{0,1:T(8,128)(2,1)S(1)}, u32[]{:S(2)}, u32[]{:S(2)}) collective-permute-start(bf16[384,576]{0,1:T(8,128)(2,1)S(1)} %copy-done.3), channel_id=1, source_target_pairs={{0,16},{16,0},{32,48},{48,32},{64,80},{80,64},{96,112},{112,96},{1... | collective-permute-start | bytes 1327112 | tf_op jit(solution)/shard_map/ppermute | solution.py:252
  36.3 42.4 %collective-permute-start.2 = (bf16[384,576]{0,1:T(8,128)(2,1)S(1)}, bf16[384,576]{0,1:T(8,128)(2,1)S(1)}, u32[]{:S(2)}, u32[]{:S(2)}) collective-permute-start(bf16[384,576]{0,1:T(8,128)(2,1)S(1)} %copy-done.2), channel_id=1, source_target_pairs={{0,16},{16,0},{32,48},{48,32},{64,80},{80,64},{96,112},{112,96},{1... | collective-permute-start | bytes 1327112 | tf_op jit(solution)/shard_map/ppermute | solution.py:253
  75.4 6.2 %copy-start = (bf16[128,960]{1,0:T(8,128)(2,1)}, bf16[128,960]{1,0:T(8,128)(2,1)S(1)}, u32[]{:S(2)}) copy-start(bf16[128,960]{1,0:T(8,128)(2,1)S(1)} %reshape.20.arrived_ref) | copy-start | bytes 737284
  75.4 5.4 %collective-permute-start = (bf16[128,384]{1,0:T(8,128)(2,1)S(1)}, bf16[128,384]{1,0:T(8,128)(2,1)S(1)}, u32[]{:S(2)}, u32[]{:S(2)}) collective-permute-start(bf16[128,384]{1,0:T(8,128)(2,1)S(1)} %slice.20), channel_id=1, source_target_pairs={{0,32},{16,48},{32,0},{48,16},{64,96},{80,112},{96,64},{112,80},{1... | collective-permute-start | bytes 294920 | tf_op jit(solution)/shard_map/ppermute | solution.py:260
  103.1 4.5 %copy-start.4 = (bf16[576,384]{1,0:T(8,128)(2,1)S(1)}, bf16[576,384]{1,0:T(8,128)(2,1)}, u32[]{:S(2)}) copy-start(bf16[576,384]{1,0:T(8,128)(2,1)} %param.25) | copy-start | bytes 1327108
  104.1 13.0 %all-to-all-start.2 = ((bf16[16,16,1152]{2,1,0:T(8,128)(2,1)}), bf16[16,16,1152]{2,1,0:T(8,128)(2,1)S(1)}, u32[]{:S(2)}, u32[]{:S(2)}) async-start(bf16[16,16,1152]{2,1,0:T(8,128)(2,1)} %broadcast_in_dim.2), calls=%async_computation.2 | async-start | bytes 1179648 | tf_op jit(solution)/shard_map/all_to_all | solution.py:275
  107.7 8.0 %collective-permute-start.3 = (bf16[576,384]{1,0:T(8,128)(2,1)S(1)}, bf16[576,384]{1,0:T(8,128)(2,1)S(1)}, u32[]{:S(2)}, u32[]{:S(2)}) collective-permute-start(bf16[576,384]{1,0:T(8,128)(2,1)S(1)} %copy-done.4), channel_id=1, source_target_pairs={{0,16},{16,0},{32,48},{48,32},{64,80},{80,64},{96,112},{112,96},{1... | collective-permute-start | bytes 1327112 | tf_op jit(solution)/shard_map/ppermute | solution.py:254
  117.6 6.5 %collective-permute-start.4 = (bf16[128,384]{1,0:T(8,128)(2,1)S(1)}, bf16[128,384]{1,0:T(8,128)(2,1)S(1)}, u32[]{:S(2)}, u32[]{:S(2)}) collective-permute-start(bf16[128,384]{1,0:T(8,128)(2,1)S(1)} %slice.24), channel_id=1, source_target_pairs={{0,32},{16,48},{32,0},{48,16},{64,96},{80,112},{96,64},{112,80},{1... | collective-permute-start | bytes 294920 | tf_op jit(solution)/shard_map/ppermute | solution.py:287
  124.9 50.3 %all-to-all-start.3 = ((bf16[64,2,896]{2,1,0:T(2,128)(2,1)}), bf16[64,2,896]{2,1,0:T(2,128)(2,1)S(1)}, u32[]{:S(2)}, u32[]{:S(2)}) async-start(bf16[64,2,896]{2,1,0:T(2,128)(2,1)} %constant_dynamic-update-slice_fusion), calls=%async_computation.3 | async-start | bytes 458752 | tf_op jit(solution)/shard_map/all_to_all | solution.py:292
  175.2 0.7 copy-start.1
